TPU v7x, 32 devices: a whole 2x2x4 slice. The times are simulated.
32 devices in a mesh: dp: 4 (over y, x), store: 8 (over z, core).
Axes of the slice: x: 2, y: 2, z: 4, core: 2. Of those that a mesh axis runs over, the one named last changes fastest.
Arguments:
- inputs: bfloat16 [4096, 1024], P(('dp', 'store')), may hold values from -6 to 6
- lengths: int32 [32], P(('dp', 'store')), may hold values from 64 to 128, as said below
- targets: int32 [4096], P('dp'), may hold values from 0 to 34303
- attn_qkv: bfloat16 [3, 1024, 1024], replicated, may hold values from -0.1875 to 0.1875
- attn_out: bfloat16 [1024, 1024], replicated, may hold values from -1 to 1
- ffn_up: bfloat16 [1024, 4096], replicated, may hold values from -0.1875 to 0.1875
- ffn_down: bfloat16 [4096, 1024], replicated, may hold values from -0.09375 to 0.09375
- norm_gains: float32 [3, 1024], replicated, may hold values from 0.25 to 1.75
- norm_shifts: float32 [3, 1024], replicated, may hold values from -1.5 to 1.5
- biases: float32 [4, 1024], replicated, may hold values from -1.5 to 1.5
- up_bias: float32 [4096], replicated, may hold values from -1.5 to 1.5
- cluster_proj: bfloat16 [1024, 2], replicated, may hold values from -0.1875 to 0.1875
- proj_first: bfloat16 [1024, 256], replicated, may hold values from -0.1875 to 0.1875
- proj_second: bfloat16 [1024, 64], replicated, may hold values from -0.1875 to 0.1875
- head_words: bfloat16 [1024, 2560], P(None, 'store'), may hold values from -0.1875 to 0.1875
- tail_first: bfloat16 [256, 5120], P(None, 'store'), may hold values from -0.375 to 0.375
- tail_second: bfloat16 [64, 26624], P(None, 'store'), may hold values from -0.75 to 0.75
- store_keys: bfloat16 [32768, 1024], P('store'), may hold values from -6 to 6
- block_rows: int32 [4, 8, 8, 128], P('dp', 'store'), may hold values from 0 to 4095
- near_slots: int32 [4, 8, 128, 8, 16], P('dp', 'store'), may hold values from 0 to 127, as said below
- near_words: int32 [4096, 128], P(('dp', 'store')), may hold values from 0 to 32703
Outputs:
- token_loss: float32 [4096], P(('dp', 'store'))
- input_grad: float32 [4096, 1024], P(('dp', 'store'))
- qkv_grad: float32 [3, 1024, 1024], P(None, 'store')
- out_grad: float32 [1024, 1024], P('store')
- up_grad: float32 [1024, 4096], P('store')
- down_grad: float32 [4096, 1024], P('store')
- gains_grad: float32 [3, 1024], P(None, 'store')
- shifts_grad: float32 [3, 1024], P(None, 'store')
- biases_grad: float32 [4, 1024], P(None, 'store')
- up_bias_grad: float32 [4096], P('store')
- cluster_grad: float32 [1024, 2], P('store')
- first_proj_grad: float32 [1024, 256], P('store')
- second_proj_grad: float32 [1024, 64], P('store')
- head_grad: float32 [1024, 2560], P(None, 'store')
- first_tail_grad: float32 [256, 5120], P(None, 'store')
- second_tail_grad: float32 [64, 26624], P(None, 'store')
Inputs may be any that keep to these rules, and one draw needn't show every extreme that they name: `lengths`: some sequence has exactly 128 tokens in every draw. `near_slots`: the 16 candidates of one token at one owner are distinct.
All inputs are finite; a program needn't handle non-finite values.
Results may differ from a plain program's by a relative error of at most 0.025.
Values may be sent and summed in bfloat16 or wider, within the bound.
No kernel may reach another device: no remote copies, remote signals or barrier semaphores. Data moves between devices by JAX's collectives and lax.ppermute only.
A program may use at most 320 MiB of HBM per device.

v0:
```python
import math

import jax
import jax.numpy as jnp
from jax import lax
from jax.experimental import pallas as pl
from jax.experimental.pallas import tpu as pltpu
from jax.sharding import Mesh
from jax.sharding import PartitionSpec as P

HEADS = 16
HD = 64


EPS = 1e-05
NEAR_WEIGHT = 0.25
NEG_FILL = -1e30
HIGH = lax.Precision.HIGHEST
STORE = ("line", "core")
LOW = jnp.bfloat16
WIDE = jnp.float32
SECOND_TILE = 256


def product(left, right):
    return jnp.dot(left, right, preferred_element_type=WIDE)


def product_tn(left, right):
    return lax.dot_general(left, right, (((0,), (0,)), ((), ())), preferred_element_type=WIDE)


def product_nt(left, right):
    return lax.dot_general(left, right, (((1,), (1,)), ((), ())), preferred_element_type=WIDE)


def norm_forward(values, gain_row, shift_row):
    row_mean = jnp.mean(values, axis=-1, keepdims=True)
    centred = values - row_mean
    inverse = lax.rsqrt(jnp.mean(centred * centred, axis=-1, keepdims=True) + EPS)
    unit_rows = centred * inverse
    return (unit_rows * gain_row + shift_row, unit_rows, inverse)


def norm_backward(grad_out, unit_rows, inverse, gain_row):
    scaled = grad_out * gain_row
    grad_in = inverse * (
        scaled
        - jnp.mean(scaled, axis=-1, keepdims=True)
        - unit_rows * jnp.mean(scaled * unit_rows, axis=-1, keepdims=True)
    )
    return (grad_in, jnp.sum(grad_out * unit_rows, axis=0, keepdims=True), jnp.sum(grad_out, axis=0, keepdims=True))


def swap_partner(value, axis, bit):
    count = lax.axis_size(axis)
    return lax.ppermute(value, axis, [(k, k ^ bit) for k in range(count)])


def after(value, *others):
    return lax.optimization_barrier((value, *others))[0]


class Halving:
    def __init__(self, blocks):
        lines = lax.axis_size("line")
        line = lax.axis_index("line")
        self.rest = blocks.shape[1:]
        self.current = blocks.reshape((lines, 2) + self.rest)
        self.steps = [(lax.axis_index("core"), "core", 1)]
        bit = 1
        while bit < lines:
            self.steps.append(((line // bit) & 1, "line", bit))
            bit *= 2
        self.received = None
        self.send()

    def send(self):
        mine, axis, bit = self.steps.pop(0)
        value = self.current
        outgoing = lax.dynamic_index_in_dim(value, 1 - mine, 1, keepdims=False).astype(LOW)
        self.outgoing = outgoing
        self.current = lax.dynamic_index_in_dim(value, mine, 1, keepdims=False)
        self.received = swap_partner(outgoing, axis, bit)

    def add(self, *others):
        received = after(self.received, *others) if others else self.received
        self.current = self.current.astype(WIDE) + received.astype(WIDE)
        if self.steps:
            self.current = self.current.reshape((-1, 2) + self.rest)
            self.send()
        return self.outgoing

    def finish(self, *others):
        while self.steps:
            self.add(*others)
        self.add(*others)
        return self.current[0].astype(LOW)


def grad_tile(left, right_parts):
    blocks = lax.axis_size("line") * 2
    right = right_parts.reshape(left.shape[0], right_parts.shape[2])
    tile = product_tn(left, right).astype(LOW)
    return tile.reshape(blocks, -1, right.shape[1])


def gather_dp(own):
    count = lax.axis_size("dp")
    return [own] + [swap_partner(own, "dp", q) for q in range(1, count)]


def join_pieces(pieces, axis, start, width, join_axis):
    count = len(pieces)
    me = lax.axis_index("dp")
    pieces = [lax.slice_in_dim(piece, start, start + width, axis=axis) for piece in pieces]
    bit = 1
    while bit < count:
        is_set = (me // bit) & 1 == 1
        pieces = [jnp.where(is_set, pieces[k ^ bit], pieces[k]) for k in range(count)]
        bit *= 2
    return jnp.concatenate([piece.astype(WIDE) for piece in pieces], axis=join_axis)


def exchange_columns(value):
    count = lax.axis_size("dp")
    tokens, columns = value.shape
    parts = value.reshape(tokens, count, columns // count).transpose(1, 0, 2)
    return lax.all_to_all(parts, "dp", 0, 0)


def cost(micros):
    return pl.CostEstimate(flops=int(micros * 9e8), transcendentals=0, bytes_accessed=1 << 20)


def head_masks(width):
    lanes = lax.broadcasted_iota(jnp.int32, (1, width), 1)
    return [(lanes // HD) % 2 == half for half in range(2)]


def masked_softmax(scores, allowed):
    scores = jnp.where(allowed, scores * HD ** (-0.5), NEG_FILL)
    exps = jnp.exp(scores - jnp.max(scores, axis=-1, keepdims=True))
    return exps / jnp.sum(exps, axis=-1, keepdims=True)


def seen_keys(tokens, length):
    rows = lax.broadcasted_iota(jnp.int32, (tokens, tokens), 0)
    cols = lax.broadcasted_iota(jnp.int32, (tokens, tokens), 1)
    return (cols <= rows) & (cols < length)


def block_kernel(
    length_ref, in_ref, qkv_ref, out_w_ref, up_bias_ref, gains_ref, shifts_ref, biases_ref,
    group_bias_ref, up_hbm, down_hbm,
    query_ref, key_ref, value_ref, mixed_ref, normed_ref, first_ref, second_ref, act_ref, sum_ref,
    hidden_ref, acc_scr, up_scr, down_scr, sems
):
    step = pl.program_id(0)
    tokens, width = in_ref.shape
    group = query_ref.shape[1]
    groups = width // group
    blocks = up_scr.shape[0]
    block = up_scr.shape[2]

    def fetches(place):
        start = place * block
        return (
            pltpu.make_async_copy(
                up_hbm.at[:, pl.ds(start, block)], up_scr.at[place], sems.at[0, place]
            ),
            pltpu.make_async_copy(
                down_hbm.at[pl.ds(start, block), :], down_scr.at[place], sems.at[1, place]
            ),
        )

    @pl.when(step == 0)
    def _():
        for place in range(blocks):
            for fetch in fetches(place):
                fetch.start()
        block_in = in_ref[...].astype(WIDE)
        normed_ref[...] = norm_forward(block_in, gains_ref[0:1], shifts_ref[0:1])[0].astype(LOW)
        acc_scr[...] = block_in + biases_ref[2:3]

    @pl.when(step < groups)
    def _():
        normed = normed_ref[...]
        query = (product(normed, qkv_ref[0]) + group_bias_ref[0:1]).astype(LOW)
        key = product(normed, qkv_ref[1]).astype(LOW)
        value = (product(normed, qkv_ref[2]) + group_bias_ref[1:2]).astype(LOW)
        query_ref[...] = query
        key_ref[...] = key
        value_ref[...] = value
        allowed = seen_keys(tokens, length_ref[0])
        masks = head_masks(128)
        zero = jnp.zeros((tokens, 128), LOW)
        for pair in range(group // 128):
            cols = slice(pair * 128, (pair + 1) * 128)
            q_pair, k_pair, v_pair = query[:, cols], key[:, cols], value[:, cols]
            mixed = jnp.zeros((tokens, 128), WIDE)
            for mask in masks:
                probs = masked_softmax(product_nt(q_pair, jnp.where(mask, k_pair, zero)), allowed)
                mixed = mixed + product(probs.astype(LOW), jnp.where(mask, v_pair, zero))
            mixed_ref[:, cols] = mixed.astype(LOW)
        acc_scr[...] += product(mixed_ref[...], out_w_ref[...])

    @pl.when(step == groups - 1)
    def _():
        first_sum = acc_scr[...]
        first_ref[...] = first_sum
        second_ref[...] = norm_forward(first_sum, gains_ref[1:2], shifts_ref[1:2])[0].astype(LOW)
        acc_scr[...] = first_sum + biases_ref[3:4]

    @pl.when(step >= groups)
    def _():
        place = step - groups
        for fetch in fetches(place):
            fetch.wait()
        pre_act = product(second_ref[...], up_scr[place]) + up_bias_ref[...]
        act = jnp.maximum(pre_act, 0.0).astype(LOW)
        act_ref[...] = act
        acc_scr[...] += product(act, down_scr[place])

    @pl.when(step == pl.num_programs(0) - 1)
    def _():
        total = acc_scr[...]
        sum_ref[...] = total
        hidden_ref[...] = norm_forward(total, gains_ref[2:3], shifts_ref[2:3])[0].astype(LOW)


def block_forward(
    length, inputs, attn_qkv, attn_out, ffn_up, ffn_down, up_bias, gains, shifts, biases
):
    tokens, width = inputs.shape
    inner = ffn_up.shape[1]
    group = min(256, width)
    groups = width // group
    block = min(1024, inner)
    blocks = inner // block
    full = pl.BlockSpec((tokens, width), lambda g, n: (0, 0))
    part = pl.BlockSpec((tokens, group), lambda g, n: (0, jnp.minimum(g, groups - 1)))
    low = jax.ShapeDtypeStruct((tokens, width), LOW)
    wide = jax.ShapeDtypeStruct((tokens, width), WIDE)
    return pl.pallas_call(
        block_kernel,
        grid_spec=pltpu.PrefetchScalarGridSpec(
            num_scalar_prefetch=1,
            grid=(groups + blocks,),
            in_specs=[
                full,
                pl.BlockSpec((3, width, group), lambda g, n: (0, 0, jnp.minimum(g, groups - 1))),
                pl.BlockSpec((group, width), lambda g, n: (jnp.minimum(g, groups - 1), 0)),
                pl.BlockSpec((1, block), lambda g, n: (0, jnp.maximum(g - groups, 0))),
                pl.BlockSpec(gains.shape, lambda g, n: (0, 0)),
                pl.BlockSpec(shifts.shape, lambda g, n: (0, 0)),
                pl.BlockSpec(biases.shape, lambda g, n: (0, 0)),
                pl.BlockSpec(
                    (biases.shape[0], group), lambda g, n: (0, jnp.minimum(g, groups - 1))
                ),
                pl.BlockSpec(memory_space=pl.ANY),
                pl.BlockSpec(memory_space=pl.ANY),
            ],
            out_specs=[part, part, part, part, full, full, full]
            + [pl.BlockSpec((tokens, block), lambda g, n: (0, jnp.maximum(g - groups, 0)))]
            + [full, full],
            scratch_shapes=[
                pltpu.VMEM((tokens, width), WIDE),
                pltpu.VMEM((blocks, width, block), LOW),
                pltpu.VMEM((blocks, block, width), LOW),
                pltpu.SemaphoreType.DMA((2, blocks)),
            ],
        ),
        out_shape=[low, low, low, low, low, wide, low]
        + [jax.ShapeDtypeStruct((tokens, inner), LOW), wide, low],
        cost_estimate=cost(16),
        name="block_forward",
    )(
        length, inputs, attn_qkv, attn_out, up_bias.reshape(1, inner), gains, shifts, biases,
        biases, ffn_up, ffn_down
    )


def norm_stats(values):
    centred = values - jnp.mean(values, axis=-1, keepdims=True)
    inverse = lax.rsqrt(jnp.mean(centred * centred, axis=-1, keepdims=True) + EPS)
    return centred * inverse, inverse


def attention_back_kernel(
    length_ref, attn_in_ref, out_w_ref, query_ref, key_ref, value_ref, parts_ref, sums_ref,
    attn_t_scr
):
    tokens = attn_in_ref.shape[0]
    width = query_ref.shape[1]

    @pl.when(pl.program_id(0) == 0)
    def _():
        attn_t_scr[...] = attn_in_ref[...].T

    mixed_grad = product(out_w_ref[...], attn_t_scr[...]).T.astype(LOW)
    allowed = seen_keys(tokens, length_ref[0])
    masks = head_masks(128)
    zero = jnp.zeros((tokens, 128), LOW)
    for pair in range(width // 128):
        cols = slice(pair * 128, (pair + 1) * 128)
        q_pair, k_pair, v_pair = query_ref[:, cols], key_ref[:, cols], value_ref[:, cols]
        m_pair = mixed_grad[:, cols]
        totals = [jnp.zeros((tokens, 128), WIDE) for _ in range(3)]
        for mask in masks:
            k_one = jnp.where(mask, k_pair, zero)
            probs = masked_softmax(product_nt(q_pair, k_one), allowed)
            prob_grad = product_nt(m_pair, jnp.where(mask, v_pair, zero))
            delta = jnp.sum(probs * prob_grad, axis=-1, keepdims=True)
            score_grad = (probs * (prob_grad - delta)).astype(LOW)
            totals[0] += product(score_grad, k_one)
            totals[1] += product_tn(score_grad, jnp.where(mask, q_pair, zero))
            totals[2] += product_tn(probs.astype(LOW), jnp.where(mask, m_pair, zero))
        for kind, total in enumerate(totals):
            scale = HD ** (-0.5) if kind < 2 else 1.0
            grad = (total * scale).astype(LOW)
            parts_ref[:, kind * width + pair * 128 : kind * width + (pair + 1) * 128] = grad
            if kind != 1:
                sums_ref[kind : kind + 1, cols] = jnp.sum(
                    grad.astype(WIDE), axis=0, keepdims=True
                )


def attention_back(length, attn_in, attn_out, query, key, value, parts):
    tokens, width = attn_in.shape
    group = width // parts
    part = pl.BlockSpec((tokens, group), lambda g, n: (0, g))
    return pl.pallas_call(
        attention_back_kernel,
        grid_spec=pltpu.PrefetchScalarGridSpec(
            num_scalar_prefetch=1,
            grid=(parts,),
            in_specs=[
                pl.BlockSpec((tokens, width), lambda g, n: (0, 0)),
                pl.BlockSpec((group, width), lambda g, n: (g, 0)),
                part,
                part,
                part,
            ],
            out_specs=[
                pl.BlockSpec((None, tokens, 3 * group), lambda g, n: (g, 0, 0)),
                pl.BlockSpec((8, group), lambda g, n: (0, g)),
            ],
            scratch_shapes=[pltpu.VMEM((width, tokens), LOW)],
        ),
        out_shape=[
            jax.ShapeDtypeStruct((parts, tokens, 3 * group), LOW),
            jax.ShapeDtypeStruct((8, width), WIDE),
        ],
        cost_estimate=cost(9),
        name="attention_back",
    )(length, attn_in, attn_out, query, key, value)


def to_columns(rows):
    short = 128 - rows.shape[0]
    padded = jnp.concatenate([rows, jnp.zeros((short, rows.shape[1]), rows.dtype)], axis=0)
    return padded.T


def word_columns(words_ref):
    columns = [to_columns(words_ref[k])[:, 0:1] for k in range(words_ref.shape[0])]
    return jnp.concatenate(columns, axis=0).astype(jnp.int32)


def is_word(where_wide, first_col):
    lanes = lax.broadcasted_iota(jnp.int32, (1, where_wide.shape[1]), 1) + first_col
    return where_wide == lanes


def stats_kernel(
    base_ref, rows_ref, words_ref, keys_ref, norms_ref, slots_ref, head_ref, first_ref,
    second_ref, proj_one_ref, proj_two_ref, stats_ref, ones_ref, twos_ref
):
    rows = rows_ref[...]
    pair = words_ref.shape[0]
    tokens = words_ref.shape[2]
    words = word_columns(words_ref)
    ones = product(rows, proj_one_ref[...]).astype(LOW)
    twos = product(rows, proj_two_ref[...]).astype(LOW)
    ones_ref[...] = ones
    twos_ref[...] = twos
    picked = jnp.zeros((rows.shape[0], 1), WIDE)
    sums = []
    for place, (left, words_w) in enumerate(
        ((rows, head_ref), (ones, first_ref), (twos, second_ref))
    ):
        columns = words_w.shape[1]
        tile = SECOND_TILE if columns % SECOND_TILE == 0 else columns
        total = jnp.zeros((rows.shape[0], tile), WIDE)
        chosen = jnp.zeros((rows.shape[0], tile), WIDE)
        where_wide = jnp.broadcast_to(words - base_ref[place], (rows.shape[0], tile))
        for start in range(0, columns, tile):
            logits = product(left, words_w[:, start : start + tile])
            total = total + jnp.exp(logits)
            chosen = jnp.where(is_word(where_wide, start), logits, chosen)
        sums.append(jnp.sum(total, axis=1, keepdims=True))
        picked = picked + jnp.sum(chosen, axis=1, keepdims=True)
    sums.append(picked)
    lanes = lax.broadcasted_iota(jnp.int32, (rows.shape[0], 128), 1)
    table = jnp.zeros((rows.shape[0], 128), WIDE)
    for place, column in enumerate(sums):
        table = jnp.where(lanes == place, column, table)
    slot_count = slots_ref.shape[1]
    scale = 1.0 / math.sqrt(rows.shape[1])
    for k in range(pair):
        keys = keys_ref[k]
        norms = norms_ref[k][:, 0:1]
        scored = product_nt(keys, rows[k * tokens : (k + 1) * tokens]) * scale
        scored = scored - norms * (0.5 * scale)
        ids = lax.broadcasted_iota(jnp.int32, scored.shape, 0)
        for m in range(slot_count):
            hit = ids == slots_ref[k, m : m + 1, :]
            stats_ref[k, m : m + 1, :] = jnp.sum(
                jnp.where(hit, scored, 0.0), axis=0, keepdims=True
            )
        stats_ref[k, slot_count : slot_count + 8, :] = table[k * tokens : (k + 1) * tokens].T[0:8]


def whole_spec(array):
    return pl.BlockSpec(array.shape, lambda *_: (0,) * array.ndim)


def word_stats(base, rows_all, words_f, key_block, norms, slots_t, weights, pair):
    sources, slot_count, tokens = slots_t.shape
    count = key_block.shape[1]
    width = rows_all.shape[1]
    chunk = pair * tokens
    ones = weights[3].shape[1]
    twos = weights[4].shape[1]
    return pl.pallas_call(
        stats_kernel,
        grid_spec=pltpu.PrefetchScalarGridSpec(
            num_scalar_prefetch=1,
            grid=(sources // pair,),
            in_specs=[
                pl.BlockSpec((chunk, width), lambda g, b: (g, 0)),
                pl.BlockSpec((pair, 1, tokens), lambda g, b: (g, 0, 0)),
                pl.BlockSpec((pair, count, width), lambda g, b: (g, 0, 0)),
                pl.BlockSpec((pair, count, 128), lambda g, b: (g, 0, 0)),
                pl.BlockSpec((pair, slot_count, tokens), lambda g, b: (g, 0, 0)),
            ]
            + [whole_spec(w) for w in weights],
            out_specs=[
                pl.BlockSpec((pair, slot_count + 8, tokens), lambda g, b: (g, 0, 0)),
                pl.BlockSpec((chunk, ones), lambda g, b: (g, 0)),
                pl.BlockSpec((chunk, twos), lambda g, b: (g, 0)),
            ],
        ),
        out_shape=[
            jax.ShapeDtypeStruct((sources, slot_count + 8, tokens), WIDE),
            jax.ShapeDtypeStruct((rows_all.shape[0], ones), LOW),
            jax.ShapeDtypeStruct((rows_all.shape[0], twos), LOW),
        ],
        cost_estimate=cost(13),
        name="word_stats",
    )(base, rows_all, words_f, key_block, norms, slots_t, *weights)


def word_grads_kernel(
    order_ref, base_ref, rows_ref, ones_ref, twos_ref, returned_ref, words_ref, keys_ref,
    slots_ref, head_ref, first_ref, second_ref, first_t_ref, second_t_ref, mixed_t_ref, *refs
):
    (
        mine_ref, other_ref, head_g_ref, first_g_ref, second_g_ref, back_ref, terms_scr, mixed_scr
    ) = refs[-8:]
    rows = rows_ref[...]
    pair = words_ref.shape[0]
    tokens = words_ref.shape[2]
    slot_count = slots_ref.shape[1]
    words = word_columns(words_ref)
    coefs = [to_columns(returned_ref[k, slot_count : slot_count + 8, :]) for k in range(pair)]
    coefs = jnp.concatenate(coefs, axis=0)
    weight = coefs[:, 0:1]
    in_first = (words >= base_ref[3]) & (words < base_ref[4])
    in_second = words >= base_ref[4]
    scales = (
        weight,
        jnp.where(in_first, weight, 0.0),
        jnp.where(in_second, weight, 0.0),
    )
    lefts = (rows, ones_ref[...], twos_ref[...])
    for place, (words_w, out_ref) in enumerate(
        ((head_ref, head_g_ref), (first_ref, first_g_ref), (second_ref, second_g_ref))
    ):
        columns = words_w.shape[1]
        tile = SECOND_TILE if columns % SECOND_TILE == 0 else columns
        where_wide = jnp.broadcast_to(words - base_ref[place], (rows.shape[0], tile))
        scale = scales[place]
        log_sum = coefs[:, place + 1 : place + 2] - jnp.log(scale)

        def one_tile(tile_w, start):
            logits = product(lefts[place], tile_w)
            hit = is_word(where_wide, start)
            return (jnp.exp(logits - log_sum) - jnp.where(hit, scale, 0.0)).astype(LOW)

        if columns == tile:
            out_ref[...] = one_tile(words_w[...], 0)
        else:

            for start in range(0, columns, tile):
                out_ref[:, start : start + tile] = one_tile(
                    words_w[:, start : start + tile], start
                )

    ones = ones_ref.shape[1]
    heads = head_g_ref.shape[1]
    mixed_scr[:, ones : ones + heads] = head_g_ref[...]
    back_one = product(first_g_ref[...], first_t_ref[...]).astype(LOW)
    mixed_scr[:, 0:ones] = back_one
    back_ref[:, 0:ones] = back_one
    back_two = product(second_g_ref[...], second_t_ref[...]).astype(LOW)
    mixed_scr[:, ones + heads :] = back_two
    back_ref[:, ones:] = back_two
    term = product(mixed_scr[...], mixed_t_ref[...])
    key_scale = 1.0 / math.sqrt(rows.shape[1])
    count = keys_ref.shape[1]
    ids = lax.broadcasted_iota(jnp.int32, (count, tokens), 0)
    for k in range(pair):
        dense = jnp.zeros((count, tokens), WIDE)
        for m in range(slot_count):
            hit = ids == slots_ref[k, m : m + 1, :]
            dense = jnp.where(hit, returned_ref[k, m : m + 1, :], dense)
        near = product_tn(dense.astype(LOW), keys_ref[k]) * key_scale
        terms_scr[k] = (term[k * tokens : (k + 1) * tokens] + near).astype(LOW)
    if pair == 2:
        core = base_ref[5]
        mine_ref[0] = terms_scr[core]
        other_ref[0] = terms_scr[1 - core]
    else:
        mine_ref[0] = terms_scr[0]
        other_ref[0] = terms_scr[0]


def word_grads(order, base, rows_all, ones_all, twos_all, returned, words_f, key_block, slots_t,
               weights, pair):
    sources, slot_count, tokens = slots_t.shape
    count = key_block.shape[1]
    width = rows_all.shape[1]
    chunk = pair * tokens
    total = rows_all.shape[0]
    steps = order.shape[0]
    sizes = [weights[k].shape[1] for k in range(3)]
    sizes.append(weights[5].shape[0] - sizes[0])

    def by_row(columns):
        return pl.BlockSpec((chunk, columns), lambda g, o, b: (o[g], 0))

    inputs = [rows_all, ones_all, twos_all, returned, words_f, key_block, slots_t, *weights]
    return pl.pallas_call(
        word_grads_kernel,
        grid_spec=pltpu.PrefetchScalarGridSpec(
            num_scalar_prefetch=2,
            grid=(steps,),
            in_specs=[
                by_row(width),
                by_row(ones_all.shape[1]),
                by_row(twos_all.shape[1]),
                pl.BlockSpec((pair, slot_count + 8, tokens), lambda g, o, b: (o[g], 0, 0)),
                pl.BlockSpec((pair, 1, tokens), lambda g, o, b: (o[g], 0, 0)),
                pl.BlockSpec((pair, count, width), lambda g, o, b: (o[g], 0, 0)),
                pl.BlockSpec((pair, slot_count, tokens), lambda g, o, b: (o[g], 0, 0)),
            ]
            + [whole_spec(w) for w in weights],
            out_specs=[
                pl.BlockSpec((1, tokens, width), lambda g, o, b: (g, 0, 0)),
                pl.BlockSpec((1, tokens, width), lambda g, o, b: (g, 0, 0)),
            ]
            + [by_row(size) for size in sizes],
            scratch_shapes=[
                pltpu.VMEM((pair, tokens, width), LOW),
                pltpu.VMEM((chunk, weights[5].shape[0]), LOW),
            ],
        ),
        out_shape=[
            jax.ShapeDtypeStruct((steps, tokens, width), LOW),
            jax.ShapeDtypeStruct((steps, tokens, width), LOW),
        ]
        + [jax.ShapeDtypeStruct((total, size), LOW) for size in sizes],
        cost_estimate=cost(10),
        name="word_grads",
    )(order, base, *inputs)


def word_sums_kernel(
    rows_ref, ones_ref, twos_ref, head_g_ref, first_g_ref, second_g_ref, back_ref,
    packed_ref, proj_ref, *scratch
):
    step = pl.program_id(0)
    pairs = (
        (head_g_ref, rows_ref),
        (ones_ref, first_g_ref),
        (twos_ref, second_g_ref),
        (rows_ref, back_ref),
    )

    @pl.when(step == 0)
    def _():
        for acc in scratch:
            acc[...] = jnp.zeros_like(acc)

    for (left, right), acc in zip(pairs, scratch):
        acc[...] += product_tn(left[...], right[...])

    @pl.when(step == pl.num_programs(0) - 1)
    def _():
        proj_ref[...] = scratch[3][...].astype(LOW)
        place = 0
        for acc in scratch[:3]:
            rows, columns = acc.shape
            for start in range(0, columns, 128):
                packed_ref[place : place + rows, :] = acc[:, start : start + 128].astype(LOW)
                place += rows


def word_sums(rows_all, ones_all, twos_all, grads):
    total = rows_all.shape[0]
    chunk = min(512, total)
    inputs = [rows_all, ones_all, twos_all, *grads]
    shapes = [
        (grads[0].shape[1], rows_all.shape[1]),
        (ones_all.shape[1], grads[1].shape[1]),
        (twos_all.shape[1], grads[2].shape[1]),
        (rows_all.shape[1], grads[3].shape[1]),
    ]
    packed_rows = sum(rows * columns for rows, columns in shapes[:3]) // 128
    out_shapes = [(packed_rows, 128), shapes[3]]
    packed, proj = pl.pallas_call(
        word_sums_kernel,
        grid=(total // chunk,),
        in_specs=[pl.BlockSpec((chunk, item.shape[1]), lambda g: (g, 0)) for item in inputs],
        out_specs=[pl.BlockSpec(shape, lambda g: (0, 0)) for shape in out_shapes],
        out_shape=[jax.ShapeDtypeStruct(shape, LOW) for shape in out_shapes],
        scratch_shapes=[pltpu.VMEM(shape, WIDE) for shape in shapes],
        cost_estimate=cost(10),
        name="word_sums",
    )(*inputs)
    return packed, proj, shapes[:3]


def unpack_kernel(me_ref, parts_ref, *outs):
    count, part_rows, _ = parts_ref.shape
    me = me_ref[0]
    place = 0
    for out in outs:
        rows, columns = out.shape
        for start in range(0, columns, 128):
            done = 0
            while done < rows:
                part, offset = divmod(place + done, part_rows)
                size = min(rows - done, part_rows - offset)
                out[done : done + size, start : start + 128] = parts_ref[
                    part ^ me, offset : offset + size, :
                ].astype(WIDE)
                done += size
            place += rows


def unpack_words(parts, shapes):
    return pl.pallas_call(
        unpack_kernel,
        grid_spec=pltpu.PrefetchScalarGridSpec(
            num_scalar_prefetch=1,
            grid=(1,),
            in_specs=[whole_spec(parts)],
            out_specs=[pl.BlockSpec(shape, lambda *_: (0, 0)) for shape in shapes],
        ),
        out_shape=[jax.ShapeDtypeStruct(shape, WIDE) for shape in shapes],
        cost_estimate=cost(3),
        compiler_params=pltpu.CompilerParams(vmem_limit_bytes=12 << 20),
        name="unpack_words",
    )(lax.axis_index("dp").astype(jnp.int32).reshape(1), parts)


def key_norms_kernel(keys_ref, norms_ref):
    for k in range(keys_ref.shape[0]):
        wide = keys_ref[k].astype(WIDE)
        norms = jnp.sum(wide * wide, axis=1, keepdims=True)
        norms_ref[k] = jnp.broadcast_to(norms, norms_ref.shape[1:])


def key_norms(key_block):
    sources, count, width = key_block.shape
    pair = min(2, sources)
    return pl.pallas_call(
        key_norms_kernel,
        grid=(sources // pair,),
        in_specs=[pl.BlockSpec((pair, count, width), lambda g: (g, 0, 0))],
        out_specs=pl.BlockSpec((pair, count, 128), lambda g: (g, 0, 0)),
        out_shape=jax.ShapeDtypeStruct((sources, count, 128), WIDE),
        cost_estimate=cost(20),
        compiler_params=pltpu.CompilerParams(vmem_limit_bytes=8 << 20),
        name="key_norms",
    )(key_block)


def input_back_kernel(
    parts_ref, qkv_ref, in_ref, grad_ref, gains_ref, input_grad_ref, sums_ref, acc_scr
):
    step = pl.program_id(0)

    @pl.when(step == 0)
    def _():
        acc_scr[...] = jnp.zeros_like(acc_scr)

    group = qkv_ref.shape[2]
    total = acc_scr[...]
    for kind in range(3):
        total = total + product(
            qkv_ref[kind], parts_ref[:, kind * group : (kind + 1) * group].T
        )
    acc_scr[...] = total

    @pl.when(step == pl.num_programs(0) - 1)
    def _():
        unit_rows, inverse = norm_stats(in_ref[...].astype(WIDE))
        back, gain, shift = norm_backward(acc_scr[...].T, unit_rows, inverse, gains_ref[0:1])
        input_grad_ref[...] = grad_ref[...] + back
        sums_ref[0:1] = gain
        sums_ref[1:2] = shift


def input_back(parts, attn_qkv, inputs, first_grad, gains):
    count, tokens, _ = parts.shape
    width = inputs.shape[1]
    group = width // count
    full = pl.BlockSpec((tokens, width), lambda g: (0, 0))
    return pl.pallas_call(
        input_back_kernel,
        grid=(count,),
        in_specs=[
            pl.BlockSpec((None, tokens, 3 * group), lambda g: (g, 0, 0)),
            pl.BlockSpec((3, width, group), lambda g: (0, 0, g)),
            full,
            full,
            pl.BlockSpec(gains.shape, lambda g: (0, 0)),
        ],
        out_specs=[full, pl.BlockSpec((8, width), lambda g: (0, 0))],
        out_shape=[
            jax.ShapeDtypeStruct((tokens, width), WIDE),
            jax.ShapeDtypeStruct((8, width), WIDE),
        ],
        scratch_shapes=[pltpu.VMEM((width, tokens), WIDE)],
        cost_estimate=cost(7),
        name="input_back",
    )(parts, attn_qkv, inputs, first_grad, gains)


def shards(
    inputs,
    lengths,
    targets,
    attn_qkv,
    attn_out,
    ffn_up,
    ffn_down,
    norm_gains,
    norm_shifts,
    biases,
    up_bias,
    cluster_proj,
    proj_first,
    proj_second,
    head_words,
    tail_first,
    tail_second,
    store_keys,
    block_rows,
    near_slots,
    near_words,
):
    tokens_here = inputs.shape[0]
    d_model = inputs.shape[1]
    dp_count = lax.axis_size("dp")
    sources = lax.axis_size("line") * 2
    my_index = lax.axis_index("line") * 2 + lax.axis_index("core")
    group_rows = tokens_here * sources
    head_cols = head_words.shape[1]
    first_cols = tail_first.shape[1]
    second_cols = tail_second.shape[1]
    head_total = head_cols * sources
    first_total = first_cols * sources
    ff_width = ffn_up.shape[1]
    valid_mask = (jnp.arange(tokens_here) < lengths[0]).astype(WIDE)

    (
        query_low, key_low, value_low, mixed_low, normed_low, first_sum, second_low, act_low,
        second_sum, hidden_low
    ) = block_forward(
        lengths, inputs, attn_qkv, attn_out, ffn_up, ffn_down, up_bias, norm_gains, norm_shifts,
        biases
    )
    cluster_logits = lax.dot_general(
        cluster_proj, hidden_low, (((0,), (1,)), ((), ())), preferred_element_type=WIDE
    )

    rows_all = lax.all_gather(hidden_low, STORE, axis=0, tiled=True)

    key_block = jnp.take(store_keys, block_rows[0, 0].reshape(-1), axis=0, mode="clip")
    key_block = key_block.reshape(sources, -1, d_model)
    slots_t = near_slots[0, 0].transpose(1, 2, 0)
    slot_count = slots_t.shape[1]
    words_t = near_words.T

    weights = (head_words, tail_first, tail_second, proj_first, proj_second)
    back_weights = weights[:3] + (
        tail_first.T,
        tail_second.T,
        jnp.concatenate([proj_first.T, head_words.T, proj_second.T], axis=0),
    )
    norms = key_norms(key_block)

    left_low = jnp.concatenate([act_low, second_low, mixed_low, normed_low], axis=1)
    left_low, rows_all, norms, slots_t, words_t, back_weights = lax.optimization_barrier(
        (left_low, rows_all, norms, slots_t, words_t, back_weights)
    )
    left_all = lax.all_gather(left_low, "dp", axis=0, tiled=True)

    core = lax.axis_index("core")
    words_f = targets.astype(WIDE).reshape(sources, 1, tokens_here)
    base = jnp.stack(
        [
            my_index * head_cols,
            head_total + my_index * first_cols,
            head_total + first_total + my_index * second_cols,
            jnp.int32(head_total),
            jnp.int32(head_total + first_total),
            core,
        ]
    ).astype(jnp.int32)
    outgoing, ones_all, twos_all = word_stats(
        base, rows_all, words_f, key_block, norms, slots_t, back_weights[:3] + weights[3:], 2
    )
    incoming = lax.all_to_all(outgoing, STORE, 0, 0)

    near_scores = incoming[:, :slot_count].reshape(sources * slot_count, tokens_here)
    own_stats = jnp.sum(incoming[:, slot_count : slot_count + 4], axis=0)
    own_words = lax.dynamic_slice_in_dim(targets, my_index * tokens_here, tokens_here, 0)
    in_first = ((own_words >= head_total) & (own_words < head_total + first_total)).astype(WIDE)
    in_second = (own_words >= head_total + first_total).astype(WIDE)
    head_sum = own_stats[0] + jnp.sum(jnp.exp(cluster_logits), axis=0)
    log_head = jnp.log(head_sum)
    log_first = jnp.log(own_stats[1])
    log_second = jnp.log(own_stats[2])
    log_model = (
        own_stats[3]
        - log_head
        + in_first * (cluster_logits[0] - log_first)
        + in_second * (cluster_logits[1] - log_second)
    )
    near_top = jnp.max(near_scores, axis=0, keepdims=True)
    near_exp = jnp.exp(near_scores - near_top)
    near_probs = near_exp / jnp.sum(near_exp, axis=0, keepdims=True)
    matched = (words_t == own_words[None, :]).astype(WIDE)
    near_mass = jnp.sum(near_probs * matched, axis=0)
    model_prob = jnp.exp(log_model)
    mixture = NEAR_WEIGHT * near_mass + (1.0 - NEAR_WEIGHT) * model_prob
    token_loss = -valid_mask * jnp.log(mixture)
    model_weight = valid_mask * (1.0 - NEAR_WEIGHT) * model_prob / mixture
    near_weight = valid_mask * NEAR_WEIGHT / mixture
    score_grad = -near_weight[None, :] * near_probs * (matched - near_mass[None, :])
    coef = jnp.stack([model_weight, log_head, log_first, log_second] + 4 * [model_weight])
    returning = jnp.concatenate(
        [
            score_grad.reshape(sources, slot_count, tokens_here),
            jnp.broadcast_to(coef[None], (sources,) + coef.shape),
        ],
        axis=1,
    )
    returned = lax.all_to_all(returning, STORE, 0, 0)

    lines = lax.axis_size("line")
    mine, other, *word_terms = word_grads(
        jnp.arange(lines, dtype=jnp.int32),
        base,
        rows_all,
        ones_all,
        twos_all,
        returned,
        words_f,
        key_block,
        slots_t,
        back_weights,
        2,
    )
    both = (mine.astype(WIDE) + swap_partner(other, "core", 1).astype(WIDE)).astype(LOW)
    row_parts = lax.all_to_all(both, "line", 0, 0)
    row_back = jnp.sum(row_parts.astype(WIDE), axis=0)
    word_terms, both = lax.optimization_barrier((word_terms, both))
    word_packed, proj_acc, word_shapes = word_sums(rows_all, ones_all, twos_all, word_terms)

    own_rows = d_model // sources
    proj_width = proj_acc.shape[1]
    sub_rows = own_rows // dp_count
    proj_parts = proj_acc.reshape(sources, dp_count, sub_rows, proj_width).transpose(1, 0, 2, 3)
    dp_index = lax.axis_index("dp")
    proj_sum = lax.dynamic_index_in_dim(proj_parts, dp_index, 0, keepdims=False).astype(WIDE)
    for q in range(1, dp_count):
        part = lax.dynamic_index_in_dim(proj_parts, dp_index ^ q, 0, keepdims=False)
        proj_sum = proj_sum + swap_partner(part, "dp", q).astype(WIDE)
    cluster_rows = model_weight[None, :] * (
        jnp.exp(cluster_logits - log_head[None, :]) - jnp.stack([in_first, in_second])
    )
    hidden_grad = row_back + lax.dot_general(
        cluster_rows, cluster_proj.astype(WIDE), (((0,), (1,)), ((), ())), precision=HIGH
    )
    cluster_acc = jnp.dot(cluster_rows, hidden_low.astype(WIDE), precision=HIGH)
    unit_three, inv_three = norm_stats(second_sum)
    second_grad, gain_three, shift_three = norm_backward(
        hidden_grad, unit_three, inv_three, norm_gains[2]
    )
    down_in = second_grad.astype(LOW)
    down_parts = exchange_columns(down_in)
    bias_down = jnp.sum(down_in.astype(WIDE), axis=0, keepdims=True)
    act_grad = product_nt(down_in, ffn_down)
    pre_grad = jnp.where(act_low.astype(WIDE) > 0, act_grad, 0.0).astype(LOW)
    up_bias_acc = jnp.sum(pre_grad.astype(WIDE), axis=0, keepdims=True)
    marks = [0, ff_width, ff_width + d_model, ff_width + 2 * d_model, ff_width + 3 * d_model]
    lefts = [left_all[:, a:b] for a, b in zip(marks[:-1], marks[1:])]
    down = Halving(grad_tile(lefts[0], after(down_parts, pre_grad)))
    norm_two_grad = product_nt(after(pre_grad, down.outgoing), ffn_up)
    unit_two, inv_two = norm_stats(first_sum)
    back_second, gain_two, shift_two = norm_backward(
        norm_two_grad, unit_two, inv_two, norm_gains[1]
    )
    first_grad_sum = second_grad + back_second
    attn_in = first_grad_sum.astype(LOW)
    bias_attn = jnp.sum(attn_in.astype(WIDE), axis=0, keepdims=True)
    mark = down.add(attn_in)
    up_width = ff_width // dp_count
    head_width = d_model // dp_count
    up_send = jnp.stack(
        [
            jnp.concatenate(
                [
                    pre_grad[:, k * up_width : (k + 1) * up_width],
                    attn_in[:, k * head_width : (k + 1) * head_width],
                ],
                axis=1,
            )
            for k in range(dp_count)
        ]
    )
    up_parts = lax.all_to_all(up_send, "dp", 0, 0)
    stacked_parts, sums_three = attention_back(
        lengths, after(attn_in, up_send, mark), attn_out, query_low, key_low, value_low, dp_count
    )
    mark = down.add(stacked_parts)
    qkv_parts = lax.all_to_all(after(stacked_parts, up_parts), "dp", 0, 0)
    word_send = after(word_packed.reshape(dp_count, -1, 128), qkv_parts)
    word_parts = lax.all_to_all(word_send, "dp", 0, 0)
    proj_rows = sub_rows * proj_width // (up_width + head_width)
    proj_block = proj_sum.astype(LOW).reshape(sources, proj_rows, up_width + head_width)
    up_parts = after(up_parts, mark)
    up = Halving(
        jnp.concatenate(
            [
                jnp.concatenate(
                    [
                        grad_tile(lefts[1], up_parts[:, :, :up_width]),
                        grad_tile(lefts[2], up_parts[:, :, up_width:]),
                    ],
                    axis=2,
                ),
                proj_block,
            ],
            axis=1,
        )
    )
    input_grad, sums_one = input_back(
        after(stacked_parts, up.outgoing, qkv_parts), attn_qkv, inputs, first_grad_sum, norm_gains
    )
    down_own = down.finish(input_grad)
    mark = up.add(input_grad, down_own)

    def by_store(value):
        rows = value.shape[0]
        return value.reshape(rows, sources, -1).transpose(1, 0, 2).reshape(sources, -1)

    small = jnp.concatenate(
        [
            by_store(jnp.concatenate([sums_one[0:1], gain_two, gain_three])),
            by_store(jnp.concatenate([sums_one[1:2], shift_two, shift_three])),
            by_store(jnp.concatenate([sums_three[0:1], sums_three[2:3], bias_attn, bias_down])),
            by_store(up_bias_acc),
            by_store(cluster_acc),
        ],
        axis=1,
    )
    small_count = small.shape[1]
    small_rows = -(-small_count // (3 * head_width))
    if own_rows % 128 == 0:
        small_rows = -(-small_rows // 8) * 8
    small = jnp.pad(small, ((0, 0), (0, small_rows * 3 * head_width - small_count)))
    small = small.reshape(sources, small_rows, 3 * head_width).astype(LOW)
    qkv = Halving(
        jnp.concatenate([grad_tile(lefts[3], after(qkv_parts, mark)), small], axis=1)
    )
    down_pieces = gather_dp(down_own)
    mark = qkv.add(qkv.outgoing)
    mark = up.add(mark)
    word_own = jnp.sum(after(word_parts, mark).astype(WIDE), axis=0).astype(LOW)
    mark = qkv.add(word_own)
    word_pieces = gather_dp(word_own)
    down_out = join_pieces(after(down_pieces, mark), 1, 0, head_width, 1)
    up_own = up.finish(down_out)
    up_pieces = gather_dp(up_own)
    word_pieces = after(word_pieces, up_own)
    head_t, first_out, second_out = unpack_words(jnp.stack(word_pieces), word_shapes)
    head_out = head_t.T
    qkv_own = qkv.finish(head_t)
    qkv_pieces = gather_dp(qkv_own)
    up_pieces = after(up_pieces, qkv_own)
    up_main = [piece[:own_rows] for piece in up_pieces]
    up_out = join_pieces(up_main, 1, 0, up_width, 1)
    out_out = join_pieces(up_main, 1, up_width, head_width, 1)
    proj_out = join_pieces(
        [piece[own_rows:].reshape(sub_rows, proj_width) for piece in up_pieces],
        0,
        0,
        sub_rows,
        0,
    )
    qkv_main = [piece[:own_rows] for piece in qkv_pieces]
    qkv_out = jnp.stack(
        [join_pieces(qkv_main, 1, kind * head_width, head_width, 1) for kind in range(3)]
    )
    small_sum = sum(piece[own_rows:].astype(WIDE) for piece in qkv_pieces).reshape(-1)
    sizes = [3 * own_rows, 3 * own_rows, 4 * own_rows, ff_width // sources, 2 * own_rows]
    ends = [0]
    for size in sizes:
        ends.append(ends[-1] + size)
    gains_out, shifts_out, biases_out, upb_out, cluster_out = (
        small_sum[a:b] for a, b in zip(ends[:-1], ends[1:])
    )
    return (
        token_loss,
        input_grad,
        qkv_out,
        out_out,
        up_out,
        down_out,
        gains_out.reshape(3, own_rows),
        shifts_out.reshape(3, own_rows),
        biases_out.reshape(4, own_rows),
        upb_out,
        cluster_out.reshape(2, own_rows).T,
        proj_out[:, : proj_first.shape[1]],
        proj_out[:, proj_first.shape[1] :],
        head_out,
        first_out,
        second_out,
    )


def solution(mesh):
    dp_count = mesh.shape["dp"]
    store_count = mesh.shape["store"]
    split = Mesh(mesh.devices.reshape(dp_count, store_count // 2, 2), ("dp",) + STORE)
    everyone = ("dp",) + STORE
    return jax.shard_map(
        shards,
        mesh=split,
        in_specs=(
            P(everyone, None),
            P(everyone),
            P("dp"),
            P(),
            P(),
            P(),
            P(),
            P(),
            P(),
            P(),
            P(),
            P(),
            P(),
            P(),
            P(None, STORE),
            P(None, STORE),
            P(None, STORE),
            P(STORE, None),
            P("dp", STORE, None, None),
            P("dp", STORE, None, None, None),
            P(everyone, None),
        ),
        out_specs=(
            P(everyone),
            P(everyone, None),
            P(None, STORE, None),
            P(STORE, None),
            P(STORE, None),
            P(STORE, None),
            P(None, STORE),
            P(None, STORE),
            P(None, STORE),
            P(STORE),
            P(STORE, None),
            P(STORE, None),
            P(STORE, None),
            P(None, STORE),
            P(None, STORE),
            P(None, STORE),
        ),
        check_vma=False,
    )
```

profile of v0, /device:TPU:0, one launch (start us, length us, event | category | flops | bytes accessed | tf_op | source)
XLA Modules:
  0.0 319.9 jit_solution(9702850818775928156)
XLA Ops:
  7.9 17.3 %block_forward.1 = (bf16[128,1024]{1,0:T(8,128)(2,1)}, bf16[128,1024]{1,0:T(8,128)(2,1)}, bf16[128,1024]{1,0:T(8,128)(2,1)}, bf16[128,1024]{1,0:T(8,128)(2,1)}, ...) custom-call(s32[1]{0:T(128)} %copy.99.length_ref, ...), custom_call_target="tpu_custom_call" | custom-call | flops 14400000000 | bytes 1048576 | tf_op jit(solution)/shard_map/block_forward/pallas_call | solution.py:245
  28.5 9.5 %gather_fusion = bf16[1024,1024]{1,0:T(8,128)(2,1)S(1)} fusion(bf16[4096,1024]{1,0:T(8,128)(2,1)} %param.38, s32[1024]{0:T(1024)S(1)} %bitcast_clamp_fusion), kind=kCustom, calls=%fused_computation | custom fusion | bytes 4198400 | tf_op jit(solution)/shard_map/jit(_take)/gather | solution.py:804
  38.1 3.2 %pad_maximum_fusion.3.mixed_t_ref = bf16[640,1024]{1,0:T(8,128)(2,1)} fusion(bf16[64,1024]{1,0:T(8,128)(2,1)S(1)} %bitcast.268, bf16[320,1024]{1,0:T(8,128)(2,1)} %bitcast.248, bf16[256,1024]{1,0:T(8,128)(2,1)} %bitcast.252), kind=kLoop, calls=%fused_computation.23 | loop fusion | flops 3932160 | bytes 2621440 | tf_op jit(solution)/shard_map/concatenate | solution.py:814
  44.2 13.1 %all-gather.3.cloned.1.call-done.rows_ref = bf16[1024,1024]{1,0:T(8,128)(2,1)} async-done(((bf16[128,1024]{1,0:T(8,128)(2,1)}), bf16[1024,1024]{1,0:T(8,128)(2,1)}) %all-gather.3.cloned.1.call-update) | async-done | bytes 2097168 | tf_op jit(solution)/shard_map/all_gather | solution.py:802
  60.6 11.7 %word_stats.1 = (f32[8,24,128]{2,1,0:T(8,128)}, bf16[1024,256]{1,0:T(8,128)(2,1)}, bf16[1024,64]{1,0:T(8,128)(2,1)}) custom-call(s32[6]{0:T(128)} %stack.94.base_ref, bf16[1024,1024]{1,0:T(8,128)(2,1)} %all-gather.3.cloned.1.call-done.rows_ref, f32[8,1,128]{2,1,0:T(1,128)} %bitcast.300, bf16[8,128,1024]{2,1,0:T(8,128)(2,1)} %bitcast.237, ...), custom_call_target="tpu_custom_call" | custom-call | flops 11699999744 | bytes 1048576 | tf_op jit(solution)/shard_map/word_stats/pallas_call | solution.py:436
  72.3 3.4 %all-to-all-start = ((f32[8,24,128]{2,1,0:T(8,128)}), f32[8,24,128]{2,1,0:T(8,128)S(1)}, u32[]{:S(2)}, u32[]{:S(2)}) async-start(f32[8,24,128]{2,1,0:T(8,128)} %get-tuple-element.101), calls=%async_computation | async-start | bytes 196608 | tf_op jit(solution)/shard_map/all_to_all | solution.py:839
  75.9 6.1 %all-to-all-done = f32[8,24,128]{2,1,0:T(8,128)S(1)} async-done(((f32[8,24,128]{2,1,0:T(8,128)}), f32[8,24,128]{2,1,0:T(8,128)S(1)}, u32[]{:S(2)}, u32[]{:S(2)}) %all-to-all-start) | async-done | bytes 98336 | tf_op jit(solution)/shard_map/all_to_all | solution.py:839
  83.9 3.5 %all-to-all-start.1 = ((f32[8,24,128]{2,1,0:T(8,128)}), f32[8,24,128]{2,1,0:T(8,128)S(1)}, u32[]{:S(2)}, u32[]{:S(2)}) async-start(f32[8,24,128]{2,1,0:T(8,128)} %pad_maximum_fusion.5), calls=%async_computation.1 | async-start | bytes 196608 | tf_op jit(solution)/shard_map/all_to_all | solution.py:875
  87.5 6.0 %all-to-all-done.1.returned_ref = f32[8,24,128]{2,1,0:T(8,128)S(1)} async-done(((f32[8,24,128]{2,1,0:T(8,128)}), f32[8,24,128]{2,1,0:T(8,128)S(1)}, u32[]{:S(2)}, u32[]{:S(2)}) %all-to-all-start.1) | async-done | bytes 98336 | tf_op jit(solution)/shard_map/all_to_all | solution.py:875
  94.2 17.9 %word_grads.1 = (bf16[4,128,1024]{2,1,0:T(8,128)(2,1)}, bf16[4,128,1024]{2,1,0:T(8,128)(2,1)}, bf16[1024,320]{1,0:T(8,128)(2,1)}, bf16[1024,640]{1,0:T(8,128)(2,...) custom-call(s32[4]{0:T(128)} %iota.7.order_ref, s32[6]{0:T(128)} %stack.94.base_ref, ...), custom_call_target="tpu_custom_call" | custom-call | flops 8999999488 | bytes 1048576 | tf_op jit(solution)/shard_map/word_grads/pallas_call | solution.py:555
  113.1 2.1 collective-permute-done
  115.1 2.9 add_convert_fusion
  118.1 4.3 %all-to-all-start.2 = ((bf16[4,128,1024]{2,1,0:T(8,128)(2,1)}), bf16[4,128,1024]{2,1,0:T(8,128)(2,1)}, u32[]{:S(2)}, u32[]{:S(2)}) async-start(bf16[4,128,1024]{2,1,0:T(8,128)(2,1)} %add_convert_fusion), calls=%async_computation.2 | async-start | bytes 2097152 | tf_op jit(solution)/shard_map/all_to_all | solution.py:892
  122.6 8.5 %word_sums.1 = (bf16[5504,128]{1,0:T(8,128)(2,1)}, bf16[1024,320]{1,0:T(8,128)(2,1)}) custom-call(bf16[1024,1024]{1,0:T(8,128)(2,1)} %all-gather.3.cloned.1.call-done.rows_ref, bf16[1024,256]{1,0:T(8,128)(2,1)} %get-tuple-element.103.ones_ref, bf16[1024,64]{1,0:T(8,128)(2,1)} %get-tuple-element.104.twos_ref, ...), custom_call_target="tpu_custom_call" | custom-call | flops 8999999488 | bytes 1048576 | tf_op jit(solution)/shard_map/word_sums/pallas_call | solution.py:633
  133.5 1.5 collective-permute-start.4
  137.2 5.0 %collective-permute-done.3 = bf16[8,32,320]{2,1,0:T(8,128)(2,1)S(1)} collective-permute-done((bf16[8,32,320]{2,1,0:T(8,128)(2,1)S(1)}, bf16[8,32,320]{2,1,0:T(8,128)(2,1)S(1)}, u32[]{:S(2)}, u32[]{:S(2)}) %collective-permute-start.3) | collective-permute-done | bytes 163872 | tf_op jit(solution)/shard_map/ppermute | solution.py:57
  142.3 4.9 %collective-permute-done.5 = bf16[8,32,320]{2,1,0:T(8,128)(2,1)} collective-permute-done((bf16[8,32,320]{2,1,0:T(8,128)(2,1)S(1)}, bf16[8,32,320]{2,1,0:T(8,128)(2,1)}, u32[]{:S(2)}, u32[]{:S(2)}) %collective-permute-start.5) | collective-permute-done | bytes 163872 | tf_op jit(solution)/shard_map/ppermute | solution.py:57
  153.9 3.6 %all-to-all-start.3 = ((bf16[4,128,256]{2,1,0:T(8,128)(2,1)}), bf16[4,128,256]{2,1,0:T(8,128)(2,1)S(1)}, u32[]{:S(2)}, u32[]{:S(2)}) async-start(bf16[4,128,256]{2,1,0:T(8,128)(2,1)} %bitcast.233), calls=%async_computation.3 | async-start | bytes 524288 | tf_op jit(solution)/shard_map/all_to_all | solution.py:129
  157.5 6.3 %fusion.40 = (bf16[4096]{0:T(1024)(128)(2,1)S(1)}, bf16[128,4096]{1,0:T(8,128)(2,1)S(1)}) fusion(bf16[128,1024]{1,0:T(8,128)(2,1)S(1)} %get-tuple-element.226, bf16[4096,1024]{1,0:T(8,128)(2,1)} %down_hbm.1, bf16[128,4096]{1,0:T(8,128)(2,1)S(1)} %copy-done.10), kind=kOutput, calls=%fused_computation.213 | convolution fusion | flops 1076359168 | bytes 10756096 | tf_op jit(solution)/shard_map/dot_general | solution.py:34
  164.0 3.5 %convolution_convert_fusion = bf16[4096,256]{1,0:T(8,128)(2,1)S(1)} fusion(bf16[512,256]{1,0:T(8,128)(2,1)S(1)} %bitcast.276, bf16[512,7168]{1,0:T(8,128)(2,1)} %all-gather.5.cloned.1.call-done), kind=kOutput, calls=%fused_computation.1 | convolution fusion | flops 1074790400 | bytes 6553600 | tf_op jit(solution)/shard_map/dot_general | solution.py:30
  169.9 6.5 %multiply_reduce_fusion.1 = (bf16[1024]{0:T(1024)(128)(2,1)S(1)}, f32[128]{0:T(128)S(1)}, f32[128]{0:T(128)S(1)}, bf16[1024]{0:T(1024)(128)(2,1)S(1)}, f32[128,1024]{1,0:T(8,128)S(1)}) fusion(f32[128,1024]{1,0:T(8,128)S(1)} %copy-done.6, f32[128]{0:T(128)S(1)} %copy-done.44, f32[128]{0:T(128)S(1)} %copy-done.36, f32[1024]{0:T(1024)S(1)} %bitcast.279, ...), kind=kOutput, calls=%fused_computation.50 | convolution fusion | flops 1074919168 | bytes 10496000 | tf_op jit(solution)/shard_map/dot_general | solution.py:34
  179.4 3.9 %all-to-all-start.4 = ((bf16[4,128,1280]{2,1,0:T(8,128)(2,1)}), bf16[4,128,1280]{2,1,0:T(8,128)(2,1)S(1)}, u32[]{:S(2)}, u32[]{:S(2)}) async-start(bf16[4,128,1280]{2,1,0:T(8,128)(2,1)} %pad_maximum_fusion.4), calls=%async_computation.4 | async-start | bytes 2621440 | tf_op jit(solution)/shard_map/all_to_all | solution.py:949
  183.3 1.8 convert_add_fusion.1
  186.0 1.5 collective-permute-start.2
  187.5 7.7 %attention_back.1 = (bf16[4,128,768]{2,1,0:T(8,128)(2,1)}, f32[8,1024]{1,0:T(8,128)}) custom-call(s32[1]{0:T(128)} %copy.99.length_ref, bf16[128,1024]{1,0:T(8,128)(2,1)} %copy-done.16, bf16[1024,1024]{1,0:T(8,128)(2,1)} %out_w_ref.3, bf16[128,1024]{1,0:T(8,128)(2,1)} %get-tuple-element.116.query_ref, bf16[128,1024]{1,0:T(8,128)(2,1)} %get-tuple-element.117.key_ref, ...), custom_call_target="tpu_custom_call" | custom-call | flops 8099999744 | bytes 1048576 | tf_op jit(solution)/shard_map/attention_back/pallas_call | solution.py:333
  195.2 5.2 %all-to-all-done.4 = bf16[4,128,1280]{2,1,0:T(8,128)(2,1)S(1)} async-done(((bf16[4,128,1280]{2,1,0:T(8,128)(2,1)}), bf16[4,128,1280]{2,1,0:T(8,128)(2,1)S(1)}, u32[]{:S(2)}, u32[]{:S(2)}) %all-to-all-start.4) | async-done | bytes 1310752 | tf_op jit(solution)/shard_map/all_to_all | solution.py:949
  200.4 4.4 %all-to-all-start.5 = ((bf16[4,128,768]{2,1,0:T(8,128)(2,1)}), bf16[4,128,768]{2,1,0:T(8,128)(2,1)}, u32[]{:S(2)}, u32[]{:S(2)}) async-start(bf16[4,128,768]{2,1,0:T(8,128)(2,1)} %get-tuple-element.132.parts_ref), calls=%async_computation.5 | async-start | bytes 1572864 | tf_op jit(solution)/shard_map/all_to_all | solution.py:954
  207.8 2.5 collective-permute-start.7
  210.3 2.6 convolution_convert_fusion.1
  212.9 1.8 convolution_convert_fusion.3
  216.1 6.5 %input_back.1 = (f32[128,1024]{1,0:T(8,128)}, f32[8,1024]{1,0:T(8,128)}) custom-call(bf16[4,128,768]{2,1,0:T(8,128)(2,1)} %get-tuple-element.132.parts_ref, bf16[3,1024,1024]{2,1,0:T(8,128)(2,1)} %qkv_ref.3, bf16[128,1024]{1,0:T(8,128)(2,1)} %in_ref.3, f32[128,1024]{1,0:T(8,128)} %get-tuple-element.224.grad_ref, f32[3,1024]{1,0:T(4,128)} %gains_ref.3), custom_call_target="tpu_custom_call" | custom-call | flops 6300000256 | bytes 1048576 | tf_op jit(solution)/shard_map/input_back/pallas_call | solution.py:733
  223.5 1.8 fusion.17
  225.4 1.6 convert_add_fusion
  228.0 2.6 convolution_convert_fusion.2
  232.1 1.5 collective-permute-start.10
  233.6 3.9 %all-to-all-start.6 = ((bf16[4,1376,128]{2,1,0:T(8,128)(2,1)}), bf16[4,1376,128]{2,1,0:T(8,128)(2,1)S(1)}, u32[]{:S(2)}, u32[]{:S(2)}) async-start(bf16[4,1376,128]{2,1,0:T(8,128)(2,1)} %bitcast.254), calls=%async_computation.6 | async-start | bytes 2818048 | tf_op jit(solution)/shard_map/all_to_all | solution.py:956
  237.5 2.0 collective-permute-start.16
  243.8 7.1 %collective-permute-done.10 = bf16[2,136,1280]{2,1,0:T(8,128)(2,1)} collective-permute-done((bf16[2,136,1280]{2,1,0:T(8,128)(2,1)}, bf16[2,136,1280]{2,1,0:T(8,128)(2,1)}, u32[]{:S(2)}, u32[]{:S(2)}) %collective-permute-start.10) | collective-permute-done | bytes 696352 | tf_op jit(solution)/shard_map/ppermute | solution.py:57
  254.1 2.3 all-to-all-done.6
  256.8 7.3 %collective-permute-done.9 = bf16[2,136,768]{2,1,0:T(8,128)(2,1)} collective-permute-done((bf16[2,136,768]{2,1,0:T(8,128)(2,1)}, bf16[2,136,768]{2,1,0:T(8,128)(2,1)}, u32[]{:S(2)}, u32[]{:S(2)}) %collective-permute-start.9) | collective-permute-done | bytes 417824 | tf_op jit(solution)/shard_map/ppermute | solution.py:57
  270.8 1.6 maximum_convert_fusion
  275.3 1.5 collective-permute-start.23
  276.8 8.7 %collective-permute-done.13 = bf16[1376,128]{1,0:T(8,128)(2,1)S(1)} collective-permute-done((bf16[1376,128]{1,0:T(8,128)(2,1)S(1)}, bf16[1376,128]{1,0:T(8,128)(2,1)S(1)}, u32[]{:S(2)}, u32[]{:S(2)}) %collective-permute-start.13) | collective-permute-done | bytes 352288 | tf_op jit(solution)/shard_map/ppermute | solution.py:57
  285.5 1.8 collective-permute-start.24
  287.5 1.6 unpack_words.1
  290.6 2.1 collective-permute-start.21
  292.7 12.3 %collective-permute-done.23 = bf16[136,1280]{1,0:T(8,128)(2,1)S(1)} collective-permute-done((bf16[136,1280]{1,0:T(8,128)(2,1)S(1)}, bf16[136,1280]{1,0:T(8,128)(2,1)S(1)}, u32[]{:S(2)}, u32[]{:S(2)}) %collective-permute-start.23) | collective-permute-done | bytes 348192 | tf_op jit(solution)/shard_map/ppermute | solution.py:57
  306.2 1.5 maximum_convert_fusion.1
  (248 shorter events, 64.4 us)
Async XLA Ops:
  7.2 68.5 %copy-start = (bf16[1024,2]{0,1:T(2,128)(2,1)S(1)}, bf16[1024,2]{0,1:T(2,128)(2,1)}, u32[]{:S(2)}) copy-start(bf16[1024,2]{0,1:T(2,128)(2,1)} %param.32) | copy-start | bytes 12292
  7.2 50.1 %all-gather.3.cloned.1.call-start = ((), (), s32[]{:S(2)}) async-start(), calls=%async_computation.7 | async-start | bytes 2359296 | tf_op jit(solution)/shard_map/all_gather | solution.py:802
  7.9 17.5 %copy-start.19 = (bf16[1024,256]{1,0:T(8,128)(2,1)S(1)}, bf16[1024,256]{1,0:T(8,128)(2,1)}, u32[]{:S(2)}) copy-start(bf16[1024,256]{1,0:T(8,128)(2,1)} %proj_one_ref.1) | copy-start | bytes 1572868
  7.9 18.5 %copy-start.20 = (bf16[64,3328]{1,0:T(8,128)(2,1)S(1)}, bf16[64,3328]{1,0:T(8,128)(2,1)}, u32[]{:S(2)}) copy-start(bf16[64,3328]{1,0:T(8,128)(2,1)} %second_ref.1) | copy-start | bytes 1277956
  25.3 138.7 %all-gather.5.cloned.1.call-start = ((), (), s32[]{:S(2)}) async-start(), calls=%async_computation.8 | async-start | bytes 9175040 | tf_op jit(solution)/shard_map/all_gather | solution.py:822
  44.2 14.0 %copy-start.32 = (s32[1024]{0:T(1024)S(1)}, s32[1024]{0:T(1024)}, u32[]{:S(2)}) copy-start(s32[1024]{0:T(1024)} %param.23) | copy-start | bytes 12292
  44.2 15.2 %copy-start.12 = (bf16[1024,320]{0,1:T(8,128)(2,1)S(1)}, bf16[1024,320]{0,1:T(8,128)(2,1)}, u32[]{:S(2)}) copy-start(bf16[1024,320]{0,1:T(8,128)(2,1)} %param.35) | copy-start | bytes 1966084
  59.4 77.0 %copy-start.33 = (pred[1,128]{1,0:T(4,128)(4,1)}, pred[1,128]{1,0:T(4,128)(4,1)S(1)}, u32[]{:S(2)}) copy-start(pred[1,128]{1,0:T(4,128)(4,1)S(1)} %get-tuple-element.228) | copy-start | bytes 388
  60.6 15.1 %copy-start.13 = (bf16[128,1024]{1,0:T(8,128)(2,1)S(1)}, bf16[128,1024]{1,0:T(8,128)(2,1)}, u32[]{:S(2)}) copy-start(bf16[128,1024]{1,0:T(8,128)(2,1)} %get-tuple-element.93) | copy-start | bytes 786436
  60.6 21.6 %copy-start.26 = (s32[128,128]{1,0:T(8,128)S(1)}, s32[128,128]{1,0:T(8,128)}, u32[]{:S(2)}) copy-start(s32[128,128]{1,0:T(8,128)} %param.41) | copy-start | bytes 196612
  60.6 26.8 %copy-start.7 = (f32[128,1024]{1,0:T(8,128)S(1)}, f32[128,1024]{1,0:T(8,128)}, u32[]{:S(2)}) copy-start(f32[128,1024]{1,0:T(8,128)} %get-tuple-element.102) | copy-start | bytes 1572868
  72.3 9.7 %all-to-all-start = ((f32[8,24,128]{2,1,0:T(8,128)}), f32[8,24,128]{2,1,0:T(8,128)S(1)}, u32[]{:S(2)}, u32[]{:S(2)}) async-start(f32[8,24,128]{2,1,0:T(8,128)} %get-tuple-element.101), calls=%async_computation | async-start | bytes 196608 | tf_op jit(solution)/shard_map/all_to_all | solution.py:839
  75.9 60.5 %copy-start.28 = (f32[2,128]{1,0:T(2,128)}, f32[2,128]{1,0:T(2,128)S(1)}, u32[]{:S(2)}) copy-start(f32[2,128]{1,0:T(2,128)S(1)} %get-tuple-element.285) | copy-start | bytes 3076
  83.2 53.2 %copy-start.30 = (f32[1,128]{1,0:T(1,128)}, f32[1,128]{1,0:T(1,128)S(1)}, u32[]{:S(2)}) copy-start(f32[1,128]{1,0:T(1,128)S(1)} %get-tuple-element.281) | copy-start | bytes 1540
  83.9 9.6 %all-to-all-start.1 = ((f32[8,24,128]{2,1,0:T(8,128)}), f32[8,24,128]{2,1,0:T(8,128)S(1)}, u32[]{:S(2)}, u32[]{:S(2)}) async-start(f32[8,24,128]{2,1,0:T(8,128)} %pad_maximum_fusion.5), calls=%async_computation.1 | async-start | bytes 196608 | tf_op jit(solution)/shard_map/all_to_all | solution.py:875
  94.2 18.0 %copy-start.6 = (f32[128,1024]{1,0:T(8,128)S(1)}, f32[128,1024]{1,0:T(8,128)}, u32[]{:S(2)}) copy-start(f32[128,1024]{1,0:T(8,128)} %get-tuple-element.110) | copy-start | bytes 1572868
  94.2 18.9 %copy-start.39 = (f32[3,1024]{1,0:T(4,128)S(1)}, f32[3,1024]{1,0:T(4,128)}, u32[]{:S(2)}) copy-start(f32[3,1024]{1,0:T(4,128)} %gains_ref.3) | copy-start | bytes 36868
  112.1 3.1 collective-permute-start
  112.5 23.9 %copy-start.42 = (pred[1,128]{1,0:T(4,128)(4,1)}, pred[1,128]{1,0:T(4,128)(4,1)S(1)}, u32[]{:S(2)}) copy-start(pred[1,128]{1,0:T(4,128)(4,1)S(1)} %compare_bitcast_fusion) | copy-start | bytes 388
  118.1 31.2 %all-to-all-start.2 = ((bf16[4,128,1024]{2,1,0:T(8,128)(2,1)}), bf16[4,128,1024]{2,1,0:T(8,128)(2,1)}, u32[]{:S(2)}, u32[]{:S(2)}) async-start(bf16[4,128,1024]{2,1,0:T(8,128)(2,1)} %add_convert_fusion), calls=%async_computation.2 | async-start | bytes 2097152 | tf_op jit(solution)/shard_map/all_to_all | solution.py:892
  132.3 10.0 %collective-permute-start.3 = (bf16[8,32,320]{2,1,0:T(8,128)(2,1)S(1)}, bf16[8,32,320]{2,1,0:T(8,128)(2,1)S(1)}, u32[]{:S(2)}, u32[]{:S(2)}) collective-permute-start(bf16[8,32,320]{2,1,0:T(8,128)(2,1)S(1)} %get-tuple-element.266), channel_id=1, source_target_pairs={{0,8},{8,0},{16,24},{24,16},{1,9},{9,1},{17,25},{25,17},{2,10},{10... | collective-permute-start | bytes 491528 | tf_op jit(solution)/shard_map/ppermute | solution.py:57
  133.5 8.8 %collective-permute-start.4 = (bf16[8,32,320]{2,1,0:T(8,128)(2,1)S(1)}, bf16[8,32,320]{2,1,0:T(8,128)(2,1)S(1)}, u32[]{:S(2)}, u32[]{:S(2)}) collective-permute-start(bf16[8,32,320]{2,1,0:T(8,128)(2,1)S(1)} %get-tuple-element.268), channel_id=1, source_target_pairs={{0,16},{8,24},{16,0},{24,8},{1,17},{9,25},{17,1},{25,9},{2,18},{10... | collective-permute-start | bytes 491528 | tf_op jit(solution)/shard_map/ppermute | solution.py:57
  135.0 12.2 %collective-permute-start.5 = (bf16[8,32,320]{2,1,0:T(8,128)(2,1)S(1)}, bf16[8,32,320]{2,1,0:T(8,128)(2,1)}, u32[]{:S(2)}, u32[]{:S(2)}) collective-permute-start(bf16[8,32,320]{2,1,0:T(8,128)(2,1)S(1)} %get-tuple-element.267), channel_id=1, source_target_pairs={{0,24},{8,16},{16,8},{24,0},{1,25},{9,17},{17,9},{25,1},{2,26},{10... | collective-permute-start | bytes 491528 | tf_op jit(solution)/shard_map/ppermute | solution.py:57
  153.9 10.1 %all-to-all-start.3 = ((bf16[4,128,256]{2,1,0:T(8,128)(2,1)}), bf16[4,128,256]{2,1,0:T(8,128)(2,1)S(1)}, u32[]{:S(2)}, u32[]{:S(2)}) async-start(bf16[4,128,256]{2,1,0:T(8,128)(2,1)} %bitcast.233), calls=%async_computation.3 | async-start | bytes 524288 | tf_op jit(solution)/shard_map/all_to_all | solution.py:129
  169.9 13.4 %collective-permute-start.1 = (bf16[4,512,256]{2,1,0:T(8,128)(2,1)}, bf16[4,512,256]{2,1,0:T(8,128)(2,1)}, u32[]{:S(2)}, u32[]{:S(2)}) collective-permute-start(bf16[4,512,256]{2,1,0:T(8,128)(2,1)} %dynamic-slice_bitcast_fusion.1), channel_id=1, source_target_pairs={{0,1},{1,0},{2,3},{3,2},{4,5},{5,4},{6,7},{7,6},{8,9},{9,8},{10,11... | collective-permute-start | bytes 3145736 | tf_op jit(solution)/shard_map/ppermute | solution.py:57
  179.4 21.0 %all-to-all-start.4 = ((bf16[4,128,1280]{2,1,0:T(8,128)(2,1)}), bf16[4,128,1280]{2,1,0:T(8,128)(2,1)S(1)}, u32[]{:S(2)}, u32[]{:S(2)}) async-start(bf16[4,128,1280]{2,1,0:T(8,128)(2,1)} %pad_maximum_fusion.4), calls=%async_computation.4 | async-start | bytes 2621440 | tf_op jit(solution)/shard_map/all_to_all | solution.py:949
  186.0 19.7 %collective-permute-start.2 = (bf16[2,512,256]{2,1,0:T(8,128)(2,1)}, bf16[2,512,256]{2,1,0:T(8,128)(2,1)}, u32[]{:S(2)}, u32[]{:S(2)}) collective-permute-start(bf16[2,512,256]{2,1,0:T(8,128)(2,1)} %fusion.11), channel_id=1, source_target_pairs={{0,2},{2,0},{4,6},{6,4},{1,3},{3,1},{5,7},{7,5},{8,10},{10,8},{12,... | collective-permute-start | bytes 1572872 | tf_op jit(solution)/shard_map/ppermute | solution.py:57
  200.4 15.6 %all-to-all-start.5 = ((bf16[4,128,768]{2,1,0:T(8,128)(2,1)}), bf16[4,128,768]{2,1,0:T(8,128)(2,1)}, u32[]{:S(2)}, u32[]{:S(2)}) async-start(bf16[4,128,768]{2,1,0:T(8,128)(2,1)} %get-tuple-element.132.parts_ref), calls=%async_computation.5 | async-start | bytes 1572864 | tf_op jit(solution)/shard_map/all_to_all | solution.py:954
  207.8 15.7 %collective-permute-start.7 = (bf16[1,512,256]{2,1,0:T(8,128)(2,1)}, bf16[1,512,256]{2,1,0:T(8,128)(2,1)S(1)}, u32[]{:S(2)}, u32[]{:S(2)}) collective-permute-start(bf16[1,512,256]{2,1,0:T(8,128)(2,1)} %dynamic-slice_convert_fusion.3), channel_id=1, source_target_pairs={{0,4},{2,6},{4,0},{6,2},{1,5},{3,7},{5,1},{7,3},{8,12},{10,14},{12... | collective-permute-start | bytes 786440 | tf_op jit(solution)/shard_map/ppermute | solution.py:57
  216.1 9.3 %collective-permute-start.6 = (bf16[4,136,1280]{2,1,0:T(8,128)(2,1)}, bf16[4,136,1280]{2,1,0:T(8,128)(2,1)}, u32[]{:S(2)}, u32[]{:S(2)}) collective-permute-start(bf16[4,136,1280]{2,1,0:T(8,128)(2,1)} %dynamic-slice_bitcast_fusion), channel_id=1, source_target_pairs={{0,1},{1,0},{2,3},{3,2},{4,5},{5,4},{6,7},{7,6},{8,9},{9,8},{10,11... | collective-permute-start | bytes 4177928 | tf_op jit(solution)/shard_map/ppermute | solution.py:57
  231.6 9.4 %collective-permute-start.8 = (bf16[4,136,768]{2,1,0:T(8,128)(2,1)}, bf16[4,136,768]{2,1,0:T(8,128)(2,1)}, u32[]{:S(2)}, u32[]{:S(2)}) collective-permute-start(bf16[4,136,768]{2,1,0:T(8,128)(2,1)} %fusion.7), channel_id=1, source_target_pairs={{0,1},{1,0},{2,3},{3,2},{4,5},{5,4},{6,7},{7,6},{8,9},{9,8},{10,11... | collective-permute-start | bytes 2506760 | tf_op jit(solution)/shard_map/ppermute | solution.py:57
  232.1 18.8 %collective-permute-start.10 = (bf16[2,136,1280]{2,1,0:T(8,128)(2,1)}, bf16[2,136,1280]{2,1,0:T(8,128)(2,1)}, u32[]{:S(2)}, u32[]{:S(2)}) collective-permute-start(bf16[2,136,1280]{2,1,0:T(8,128)(2,1)} %fusion.10), channel_id=1, source_target_pairs={{0,2},{2,0},{4,6},{6,4},{1,3},{3,1},{5,7},{7,5},{8,10},{10,8},{12,... | collective-permute-start | bytes 2088968 | tf_op jit(solution)/shard_map/ppermute | solution.py:57
  233.6 22.8 %all-to-all-start.6 = ((bf16[4,1376,128]{2,1,0:T(8,128)(2,1)}), bf16[4,1376,128]{2,1,0:T(8,128)(2,1)S(1)}, u32[]{:S(2)}, u32[]{:S(2)}) async-start(bf16[4,1376,128]{2,1,0:T(8,128)(2,1)} %bitcast.254), calls=%async_computation.6 | async-start | bytes 2818048 | tf_op jit(solution)/shard_map/all_to_all | solution.py:956
  237.5 29.5 %collective-permute-start.16 = (bf16[512,256]{1,0:T(8,128)(2,1)}, bf16[512,256]{1,0:T(8,128)(2,1)}, u32[]{:S(2)}, u32[]{:S(2)}) collective-permute-start(bf16[512,256]{1,0:T(8,128)(2,1)} %fusion.17), channel_id=1, source_target_pairs={{0,8},{8,0},{16,24},{24,16},{1,9},{9,1},{17,25},{25,17},{2,10},{10... | collective-permute-start | bytes 786440 | tf_op jit(solution)/shard_map/ppermute | solution.py:57
  239.5 28.1 %collective-permute-start.17 = (bf16[512,256]{1,0:T(8,128)(2,1)}, bf16[512,256]{1,0:T(8,128)(2,1)}, u32[]{:S(2)}, u32[]{:S(2)}) collective-permute-start(bf16[512,256]{1,0:T(8,128)(2,1)} %fusion.17), channel_id=1, source_target_pairs={{0,16},{8,24},{16,0},{24,8},{1,17},{9,25},{17,1},{25,9},{2,18},{10... | collective-permute-start | bytes 786440 | tf_op jit(solution)/shard_map/ppermute | solution.py:57
  241.0 28.1 %collective-permute-start.18 = (bf16[512,256]{1,0:T(8,128)(2,1)}, bf16[512,256]{1,0:T(8,128)(2,1)}, u32[]{:S(2)}, u32[]{:S(2)}) collective-permute-start(bf16[512,256]{1,0:T(8,128)(2,1)} %fusion.17), channel_id=1, source_target_pairs={{0,24},{8,16},{16,8},{24,0},{1,25},{9,17},{17,9},{25,1},{2,26},{10... | collective-permute-start | bytes 786440 | tf_op jit(solution)/shard_map/ppermute | solution.py:57
  243.3 20.9 %collective-permute-start.9 = (bf16[2,136,768]{2,1,0:T(8,128)(2,1)}, bf16[2,136,768]{2,1,0:T(8,128)(2,1)}, u32[]{:S(2)}, u32[]{:S(2)}) collective-permute-start(bf16[2,136,768]{2,1,0:T(8,128)(2,1)} %fusion.12), channel_id=1, source_target_pairs={{0,2},{2,0},{4,6},{6,4},{1,3},{3,1},{5,7},{7,5},{8,10},{10,8},{12,... | collective-permute-start | bytes 1253384 | tf_op jit(solution)/shard_map/ppermute | solution.py:57
  252.9 19.5 %collective-permute-start.15 = (bf16[1,136,1280]{2,1,0:T(8,128)(2,1)}, bf16[1,136,1280]{2,1,0:T(8,128)(2,1)}, u32[]{:S(2)}, u32[]{:S(2)}) collective-permute-start(bf16[1,136,1280]{2,1,0:T(8,128)(2,1)} %dynamic-slice_convert_fusion.2), channel_id=1, source_target_pairs={{0,4},{2,6},{4,0},{6,2},{1,5},{3,7},{5,1},{7,3},{8,12},{10,14},{12... | collective-permute-start | bytes 1044488 | tf_op jit(solution)/shard_map/ppermute | solution.py:57
  264.2 11.2 %collective-permute-start.12 = (bf16[1376,128]{1,0:T(8,128)(2,1)S(1)}, bf16[1376,128]{1,0:T(8,128)(2,1)S(1)}, u32[]{:S(2)}, u32[]{:S(2)}) collective-permute-start(bf16[1376,128]{1,0:T(8,128)(2,1)S(1)} %reduce_sum.215), channel_id=1, source_target_pairs={{0,8},{8,0},{16,24},{24,16},{1,9},{9,1},{17,25},{25,17},{2,10},{10... | collective-permute-start | bytes 1056776 | tf_op jit(solution)/shard_map/ppermute | solution.py:57
  267.0 18.6 %collective-permute-start.13 = (bf16[1376,128]{1,0:T(8,128)(2,1)S(1)}, bf16[1376,128]{1,0:T(8,128)(2,1)S(1)}, u32[]{:S(2)}, u32[]{:S(2)}) collective-permute-start(bf16[1376,128]{1,0:T(8,128)(2,1)S(1)} %reduce_sum.215), channel_id=1, source_target_pairs={{0,16},{8,24},{16,0},{24,8},{1,17},{9,25},{17,1},{25,9},{2,18},{10... | collective-permute-start | bytes 1056776 | tf_op jit(solution)/shard_map/ppermute | solution.py:57
  267.7 19.6 %collective-permute-start.14 = (bf16[1376,128]{1,0:T(8,128)(2,1)S(1)}, bf16[1376,128]{1,0:T(8,128)(2,1)S(1)}, u32[]{:S(2)}, u32[]{:S(2)}) collective-permute-start(bf16[1376,128]{1,0:T(8,128)(2,1)S(1)} %reduce_sum.215), channel_id=1, source_target_pairs={{0,24},{8,16},{16,8},{24,0},{1,25},{9,17},{17,9},{25,1},{2,26},{10... | collective-permute-start | bytes 1056776 | tf_op jit(solution)/shard_map/ppermute | solution.py:57
  269.1 20.0 %collective-permute-start.11 = (bf16[1,136,768]{2,1,0:T(8,128)(2,1)S(1)}, bf16[1,136,768]{2,1,0:T(8,128)(2,1)S(1)}, u32[]{:S(2)}, u32[]{:S(2)}) collective-permute-start(bf16[1,136,768]{2,1,0:T(8,128)(2,1)S(1)} %dynamic-slice_convert_fusion.4), channel_id=1, source_target_pairs={{0,4},{2,6},{4,0},{6,2},{1,5},{3,7},{5,1},{7,3},{8,12},{10,14},{12... | collective-permute-start | bytes 626696 | tf_op jit(solution)/shard_map/ppermute | solution.py:57
  273.5 17.1 %collective-permute-start.22 = (bf16[136,1280]{1,0:T(8,128)(2,1)S(1)}, bf16[136,1280]{1,0:T(8,128)(2,1)S(1)}, u32[]{:S(2)}, u32[]{:S(2)}) collective-permute-start(bf16[136,1280]{1,0:T(8,128)(2,1)S(1)} %fusion.16), channel_id=1, source_target_pairs={{0,8},{8,0},{16,24},{24,16},{1,9},{9,1},{17,25},{25,17},{2,10},{10... | collective-permute-start | bytes 1044488 | tf_op jit(solution)/shard_map/ppermute | solution.py:57
  275.3 29.6 %collective-permute-start.23 = (bf16[136,1280]{1,0:T(8,128)(2,1)S(1)}, bf16[136,1280]{1,0:T(8,128)(2,1)S(1)}, u32[]{:S(2)}, u32[]{:S(2)}) collective-permute-start(bf16[136,1280]{1,0:T(8,128)(2,1)S(1)} %fusion.16), channel_id=1, source_target_pairs={{0,16},{8,24},{16,0},{24,8},{1,17},{9,25},{17,1},{25,9},{2,18},{10... | collective-permute-start | bytes 1044488 | tf_op jit(solution)/shard_map/ppermute | solution.py:57
  285.5 19.4 %collective-permute-start.24 = (bf16[136,1280]{1,0:T(8,128)(2,1)S(1)}, bf16[136,1280]{1,0:T(8,128)(2,1)S(1)}, u32[]{:S(2)}, u32[]{:S(2)}) collective-permute-start(bf16[136,1280]{1,0:T(8,128)(2,1)S(1)} %fusion.16), channel_id=1, source_target_pairs={{0,24},{8,16},{16,8},{24,0},{1,25},{9,17},{17,9},{25,1},{2,26},{10... | collective-permute-start | bytes 1044488 | tf_op jit(solution)/shard_map/ppermute | solution.py:57
  289.1 20.1 %collective-permute-start.19 = (bf16[136,768]{1,0:T(8,128)(2,1)S(1)}, bf16[136,768]{1,0:T(8,128)(2,1)S(1)}, u32[]{:S(2)}, u32[]{:S(2)}) collective-permute-start(bf16[136,768]{1,0:T(8,128)(2,1)S(1)} %bitcast.260), channel_id=1, source_target_pairs={{0,24},{8,16},{16,8},{24,0},{1,25},{9,17},{17,9},{25,1},{2,26},{10... | collective-permute-start | bytes 626696 | tf_op jit(solution)/shard_map/ppermute | solution.py:57
  290.4 18.9 %collective-permute-start.20 = (bf16[136,768]{1,0:T(8,128)(2,1)S(1)}, bf16[136,768]{1,0:T(8,128)(2,1)S(1)}, u32[]{:S(2)}, u32[]{:S(2)}) collective-permute-start(bf16[136,768]{1,0:T(8,128)(2,1)S(1)} %bitcast.261), channel_id=1, source_target_pairs={{0,16},{8,24},{16,0},{24,8},{1,17},{9,25},{17,1},{25,9},{2,18},{10... | collective-permute-start | bytes 626696 | tf_op jit(solution)/shard_map/ppermute | solution.py:57
  290.6 18.7 %collective-permute-start.21 = (bf16[136,768]{1,0:T(8,128)(2,1)S(1)}, bf16[136,768]{1,0:T(8,128)(2,1)S(1)}, u32[]{:S(2)}, u32[]{:S(2)}) collective-permute-start(bf16[136,768]{1,0:T(8,128)(2,1)S(1)} %bitcast.262), channel_id=1, source_target_pairs={{0,8},{8,0},{16,24},{24,16},{1,9},{9,1},{17,25},{25,17},{2,10},{10... | collective-permute-start | bytes 626696 | tf_op jit(solution)/shard_map/ppermute | solution.py:57
  (32 other events, 167.2 us)
Sparse Core Ops, SparseCore 0:
  25.4 31.7 all-gather.2
  59.7 81.0 all-gather.4
where the time goes:
time: 322 us; the launch traced here: 320 us
  waiting for transfers between devices  81 us (25%)
  Pallas kernels  72 us (22%)
  starting transfers between devices  53.8 us (17%)
  other arithmetic  39.1 us (12%)
  local copies, waits for them, and re-layouts  32.8 us (10%)
  matrix products  25.6 us (8%)
  between operations  15.7 us (5%)
    ppermute x25, waiting for transfers between devices, swap_partner(): return lax.ppermute(value, axis, [(k, k ^ bit) for k in range(count)])  48.3 us
    ppermute x25, starting transfers between devices, swap_partner(): return lax.ppermute(value, axis, [(k, k ^ bit) for k in range(count)])  26.7 us
    pallas_call x1, Pallas kernels, word_grads(): pl.pallas_call(word_grads_kernel, grid_spec=pltpu.PrefetchScalarGridSpec(...  17.9 us
    pallas_call x1, Pallas kernels, block_forward(): pl.pallas_call(block_kernel, grid_spec=pltpu.PrefetchScalarGridSpec(num_s...  17.3 us
    all_gather x1, waiting for transfers between devices, shards(): rows_all = lax.all_gather(hidden_low, STORE, axis=0, tiled=True)  13.1 us
    dot_general x2, matrix products, product_nt(): lax.dot_general(left, right, (((1,), (1,)), ((), ())), preferred_element_...  12.8 us
    pallas_call x1, Pallas kernels, word_stats(): pl.pallas_call(stats_kernel, grid_spec=pltpu.PrefetchScalarGridSpec(num_s...  11.7 us
    dot_general x4, matrix products, product_tn(): lax.dot_general(left, right, (((0,), (0,)), ((), ())), preferred_element_...  10.4 us
  transfers between devices with their start and end apart: 34, of which 13 were waited for; matrix products, arithmetic and copies ran while one was open for 25% of the time, Pallas kernels for 17%

commit v1 on v0

--- a/solution.py
+++ b/solution.py
@@ -353,6 +353,7 @@
             jax.ShapeDtypeStruct((8, width), WIDE),
         ],
         cost_estimate=cost(9),
+        compiler_params=pltpu.CompilerParams(vmem_limit_bytes=10 << 20),
         name="attention_back",
     )(length, attn_in, attn_out, query, key, value)
 
@@ -747,6 +748,7 @@
         ],
         scratch_shapes=[pltpu.VMEM((width, tokens), WIDE)],
         cost_estimate=cost(7),
+        compiler_params=pltpu.CompilerParams(vmem_limit_bytes=12 << 20),
         name="input_back",
     )(parts, attn_qkv, inputs, first_grad, gains)
 

time: 322 us -> 320 us (level)
  local copies, waits for them, and re-layouts: 32.8 us -> 40.5 us
  other arithmetic: 39.1 us -> 33.9 us
  waiting for transfers between devices: 81 us -> 77.4 us
  starting transfers between devices: 53.8 us -> 57.3 us
    unnamed x97 -> x91, local copies, waits for them, and re-layouts: 7.68 us -> 15.4 us
    ppermute x25, waiting for transfers between devices: 48.3 us -> 42.5 us  [swap_partner(): return lax.ppermute(value, axis, [(k, k ^ bit) for k in range(count)])]
    ppermute x25, starting transfers between devices: 26.7 us -> 30.1 us  [swap_partner(): return lax.ppermute(value, axis, [(k, k ^ bit) for k in range(count)])]
  transfers between devices with their start and end apart: 34 -> 34, of which waited for: 13 -> 14; matrix products, arithmetic and copies ran while one was open for 25% -> 23% of each run, Pallas kernels for 17% -> 16%
where the time goes in v1:
time: 320 us; the launch traced here: 319 us
  waiting for transfers between devices  77.4 us (24%)
  Pallas kernels  69.7 us (22%)
  starting transfers between devices  57.3 us (18%)
  local copies, waits for them, and re-layouts  40.5 us (13%)
  other arithmetic  33.9 us (11%)
  matrix products  24.1 us (8%)
  between operations  15.7 us (5%)
    ppermute x25, waiting for transfers between devices, swap_partner(): return lax.ppermute(value, axis, [(k, k ^ bit) for k in range(count)])  42.5 us
    ppermute x25, starting transfers between devices, swap_partner(): return lax.ppermute(value, axis, [(k, k ^ bit) for k in range(count)])  30.1 us
    pallas_call x1, Pallas kernels, word_grads(): pl.pallas_call(word_grads_kernel, grid_spec=pltpu.PrefetchScalarGridSpec(...  17.9 us
    pallas_call x1, Pallas kernels, block_forward(): pl.pallas_call(block_kernel, grid_spec=pltpu.PrefetchScalarGridSpec(num_s...  17.3 us
    unnamed x91, local copies, waits for them, and re-layouts  15.4 us
    all_gather x1, waiting for transfers between devices, shards(): rows_all = lax.all_gather(hidden_low, STORE, axis=0, tiled=True)  13.1 us
    dot_general x2, matrix products, product_nt(): lax.dot_general(left, right, (((1,), (1,)), ((), ())), preferred_element_...  12.8 us
    pallas_call x1, Pallas kernels, word_stats(): pl.pallas_call(stats_kernel, grid_spec=pltpu.PrefetchScalarGridSpec(num_s...  11.7 us
  transfers between devices with their start and end apart: 34, of which 14 were waited for; matrix products, arithmetic and copies ran while one was open for 23% of the time, Pallas kernels for 16%

profile of v1, /device:TPU:0, one launch (start us, length us, event | category | flops | bytes accessed | tf_op | source)
XLA Modules:
  0.0 318.6 jit_solution(9498003212519693975)
XLA Ops:
  7.9 17.3 %block_forward.1 = (bf16[128,1024]{1,0:T(8,128)(2,1)}, bf16[128,1024]{1,0:T(8,128)(2,1)}, bf16[128,1024]{1,0:T(8,128)(2,1)}, bf16[128,1024]{1,0:T(8,128)(2,1)}, ...) custom-call(s32[1]{0:T(128)} %copy.99.length_ref, ...), custom_call_target="tpu_custom_call" | custom-call | flops 14400000000 | bytes 1048576 | tf_op jit(solution)/shard_map/block_forward/pallas_call | solution.py:245
  28.5 9.5 %gather_fusion = bf16[1024,1024]{1,0:T(8,128)(2,1)S(1)} fusion(bf16[4096,1024]{1,0:T(8,128)(2,1)} %param.38, s32[1024]{0:T(1024)S(1)} %bitcast_clamp_fusion), kind=kCustom, calls=%fused_computation | custom fusion | bytes 4198400 | tf_op jit(solution)/shard_map/jit(_take)/gather | solution.py:806
  38.1 3.2 %pad_maximum_fusion.3.mixed_t_ref = bf16[640,1024]{1,0:T(8,128)(2,1)} fusion(bf16[64,1024]{1,0:T(8,128)(2,1)S(1)} %bitcast.267, bf16[320,1024]{1,0:T(8,128)(2,1)} %bitcast.247, bf16[256,1024]{1,0:T(8,128)(2,1)} %bitcast.251), kind=kLoop, calls=%fused_computation.23 | loop fusion | flops 3932160 | bytes 2621440 | tf_op jit(solution)/shard_map/concatenate | solution.py:816
  44.2 13.1 %all-gather.3.cloned.1.call-done.rows_ref = bf16[1024,1024]{1,0:T(8,128)(2,1)} async-done(((bf16[128,1024]{1,0:T(8,128)(2,1)}), bf16[1024,1024]{1,0:T(8,128)(2,1)}) %all-gather.3.cloned.1.call-update) | async-done | bytes 2097168 | tf_op jit(solution)/shard_map/all_gather | solution.py:804
  60.6 11.7 %word_stats.1 = (f32[8,24,128]{2,1,0:T(8,128)}, bf16[1024,256]{1,0:T(8,128)(2,1)}, bf16[1024,64]{1,0:T(8,128)(2,1)}) custom-call(s32[6]{0:T(128)} %stack.94.base_ref, bf16[1024,1024]{1,0:T(8,128)(2,1)} %all-gather.3.cloned.1.call-done.rows_ref, f32[8,1,128]{2,1,0:T(1,128)} %bitcast.300, bf16[8,128,1024]{2,1,0:T(8,128)(2,1)} %bitcast.237, ...), custom_call_target="tpu_custom_call" | custom-call | flops 11699999744 | bytes 1048576 | tf_op jit(solution)/shard_map/word_stats/pallas_call | solution.py:437
  72.3 3.4 %all-to-all-start = ((f32[8,24,128]{2,1,0:T(8,128)}), f32[8,24,128]{2,1,0:T(8,128)S(1)}, u32[]{:S(2)}, u32[]{:S(2)}) async-start(f32[8,24,128]{2,1,0:T(8,128)} %get-tuple-element.101), calls=%async_computation | async-start | bytes 196608 | tf_op jit(solution)/shard_map/all_to_all | solution.py:841
  75.9 6.1 %all-to-all-done = f32[8,24,128]{2,1,0:T(8,128)S(1)} async-done(((f32[8,24,128]{2,1,0:T(8,128)}), f32[8,24,128]{2,1,0:T(8,128)S(1)}, u32[]{:S(2)}, u32[]{:S(2)}) %all-to-all-start) | async-done | bytes 98336 | tf_op jit(solution)/shard_map/all_to_all | solution.py:841
  83.8 3.5 %all-to-all-start.1 = ((f32[8,24,128]{2,1,0:T(8,128)}), f32[8,24,128]{2,1,0:T(8,128)S(1)}, u32[]{:S(2)}, u32[]{:S(2)}) async-start(f32[8,24,128]{2,1,0:T(8,128)} %pad_maximum_fusion.5), calls=%async_computation.1 | async-start | bytes 196608 | tf_op jit(solution)/shard_map/all_to_all | solution.py:877
  87.5 6.0 %all-to-all-done.1.returned_ref = f32[8,24,128]{2,1,0:T(8,128)S(1)} async-done(((f32[8,24,128]{2,1,0:T(8,128)}), f32[8,24,128]{2,1,0:T(8,128)S(1)}, u32[]{:S(2)}, u32[]{:S(2)}) %all-to-all-start.1) | async-done | bytes 98336 | tf_op jit(solution)/shard_map/all_to_all | solution.py:877
  94.1 17.9 %word_grads.1 = (bf16[4,128,1024]{2,1,0:T(8,128)(2,1)}, bf16[4,128,1024]{2,1,0:T(8,128)(2,1)}, bf16[1024,320]{1,0:T(8,128)(2,1)}, bf16[1024,640]{1,0:T(8,128)(2,...) custom-call(s32[4]{0:T(128)} %iota.7.order_ref, s32[6]{0:T(128)} %stack.94.base_ref, ...), custom_call_target="tpu_custom_call" | custom-call | flops 8999999488 | bytes 1048576 | tf_op jit(solution)/shard_map/word_grads/pallas_call | solution.py:556
  112.5 2.5 collective-permute-done
  115.0 2.6 add_convert_fusion
  117.6 3.5 %all-to-all-start.2 = ((bf16[4,128,1024]{2,1,0:T(8,128)(2,1)}), bf16[4,128,1024]{2,1,0:T(8,128)(2,1)S(1)}, u32[]{:S(2)}, u32[]{:S(2)}) async-start(bf16[4,128,1024]{2,1,0:T(8,128)(2,1)} %add_convert_fusion), calls=%async_computation.2 | async-start | bytes 2097152 | tf_op jit(solution)/shard_map/all_to_all | solution.py:894
  121.3 8.5 %word_sums.1 = (bf16[5504,128]{1,0:T(8,128)(2,1)}, bf16[1024,320]{1,0:T(8,128)(2,1)}) custom-call(bf16[1024,1024]{1,0:T(8,128)(2,1)} %all-gather.3.cloned.1.call-done.rows_ref, bf16[1024,256]{1,0:T(8,128)(2,1)} %get-tuple-element.103.ones_ref, bf16[1024,64]{1,0:T(8,128)(2,1)} %get-tuple-element.104.twos_ref, ...), custom_call_target="tpu_custom_call" | custom-call | flops 8999999488 | bytes 1048576 | tf_op jit(solution)/shard_map/word_sums/pallas_call | solution.py:634
  129.9 1.9 dynamic-slice_bitcast_fusion.4
  135.5 6.8 %collective-permute-done.3 = bf16[8,32,320]{2,1,0:T(8,128)(2,1)} collective-permute-done((bf16[8,32,320]{2,1,0:T(8,128)(2,1)}, bf16[8,32,320]{2,1,0:T(8,128)(2,1)}, u32[]{:S(2)}, u32[]{:S(2)}) %collective-permute-start.3) | collective-permute-done | bytes 163872 | tf_op jit(solution)/shard_map/ppermute | solution.py:57
  142.4 4.8 %collective-permute-done.5 = bf16[8,32,320]{2,1,0:T(8,128)(2,1)} collective-permute-done((bf16[8,32,320]{2,1,0:T(8,128)(2,1)}, bf16[8,32,320]{2,1,0:T(8,128)(2,1)}, u32[]{:S(2)}, u32[]{:S(2)}) %collective-permute-start.5) | collective-permute-done | bytes 163872 | tf_op jit(solution)/shard_map/ppermute | solution.py:57
  152.1 3.6 %all-to-all-start.3 = ((bf16[4,128,256]{2,1,0:T(8,128)(2,1)}), bf16[4,128,256]{2,1,0:T(8,128)(2,1)S(1)}, u32[]{:S(2)}, u32[]{:S(2)}) async-start(bf16[4,128,256]{2,1,0:T(8,128)(2,1)} %bitcast.233), calls=%async_computation.3 | async-start | bytes 524288 | tf_op jit(solution)/shard_map/all_to_all | solution.py:129
  155.7 6.3 %fusion.40 = (bf16[4096]{0:T(1024)(128)(2,1)S(1)}, bf16[128,4096]{1,0:T(8,128)(2,1)S(1)}) fusion(bf16[128,1024]{1,0:T(8,128)(2,1)S(1)} %get-tuple-element.226, bf16[4096,1024]{1,0:T(8,128)(2,1)} %down_hbm.1, bf16[128,4096]{1,0:T(8,128)(2,1)S(1)} %copy-done.20), kind=kOutput, calls=%fused_computation.213 | convolution fusion | flops 1076359168 | bytes 10756096 | tf_op jit(solution)/shard_map/dot_general | solution.py:34
  163.0 3.5 %convolution_convert_fusion = bf16[4096,256]{1,0:T(8,128)(2,1)S(1)} fusion(bf16[512,256]{1,0:T(8,128)(2,1)S(1)} %bitcast.275, bf16[512,7168]{1,0:T(8,128)(2,1)} %all-gather.5.cloned.1.call-done), kind=kOutput, calls=%fused_computation.1 | convolution fusion | flops 1074790400 | bytes 6553600 | tf_op jit(solution)/shard_map/dot_general | solution.py:30
  167.9 6.5 %multiply_reduce_fusion.1 = (bf16[1024]{0:T(1024)(128)(2,1)S(1)}, f32[128]{0:T(128)S(1)}, f32[128]{0:T(128)S(1)}, bf16[1024]{0:T(1024)(128)(2,1)S(1)}, f32[128,1024]{1,0:T(8,128)S(1)}) fusion(f32[128,1024]{1,0:T(8,128)S(1)} %copy-done.13, f32[128]{0:T(128)S(1)} %add_rsqrt_fusion, f32[128]{0:T(128)S(1)} %broadcast_multiply_fusion.2, f32[1024]{0:T(1024)S(1)} %bitcast.279, ...), kind=kOutput, calls=%fused_computation.50 | convolution fusion | flops 1074919168 | bytes 10496000 | tf_op jit(solution)/shard_map/dot_general | solution.py:34
  176.8 4.3 %all-to-all-start.4 = ((bf16[4,128,1280]{2,1,0:T(8,128)(2,1)}), bf16[4,128,1280]{2,1,0:T(8,128)(2,1)}, u32[]{:S(2)}, u32[]{:S(2)}) async-start(bf16[4,128,1280]{2,1,0:T(8,128)(2,1)} %pad_maximum_fusion.4), calls=%async_computation.4 | async-start | bytes 2621440 | tf_op jit(solution)/shard_map/all_to_all | solution.py:951
  181.2 1.9 convert_add_fusion.1
  185.5 6.5 %attention_back.1 = (bf16[4,128,768]{2,1,0:T(8,128)(2,1)}, f32[8,1024]{1,0:T(8,128)S(1)}) custom-call(s32[1]{0:T(128)} %copy.99.length_ref, bf16[128,1024]{1,0:T(8,128)(2,1)S(1)} %get-tuple-element.115.attn_in_ref, bf16[1024,1024]{1,0:T(8,128)(2,1)S(1)} %copy-done.5, bf16[128,1024]{1,0:T(8,128)(2,1)S(1)} %copy-done.8, bf16[128,1024]{1,0:T(8,128)(2,1)S(1)} %copy-done.9, ...), custom_call_target="tpu_custom_call" | custom-call | flops 8099999744 | bytes 1048576 | tf_op jit(solution)/shard_map/attention_back/pallas_call | solution.py:333
  191.9 6.7 %all-to-all-done.4 = bf16[4,128,1280]{2,1,0:T(8,128)(2,1)} async-done(((bf16[4,128,1280]{2,1,0:T(8,128)(2,1)}), bf16[4,128,1280]{2,1,0:T(8,128)(2,1)}, u32[]{:S(2)}, u32[]{:S(2)}) %all-to-all-start.4) | async-done | bytes 1310752 | tf_op jit(solution)/shard_map/all_to_all | solution.py:951
  198.6 4.4 %all-to-all-start.5 = ((bf16[4,128,768]{2,1,0:T(8,128)(2,1)}), bf16[4,128,768]{2,1,0:T(8,128)(2,1)}, u32[]{:S(2)}, u32[]{:S(2)}) async-start(bf16[4,128,768]{2,1,0:T(8,128)(2,1)} %get-tuple-element.132.parts_ref), calls=%async_computation.5 | async-start | bytes 1572864 | tf_op jit(solution)/shard_map/all_to_all | solution.py:956
  207.6 2.5 collective-permute-start.7
  210.0 2.5 convolution_convert_fusion.1
  212.6 1.7 convolution_convert_fusion.3
  214.6 1.6 copy-done.11
  217.2 2.8 copy-done.4
  220.0 5.4 %input_back.1 = (f32[128,1024]{1,0:T(8,128)}, f32[8,1024]{1,0:T(8,128)S(1)}) custom-call(bf16[4,128,768]{2,1,0:T(8,128)(2,1)} %get-tuple-element.132.parts_ref, bf16[3,1024,1024]{2,1,0:T(8,128)(2,1)S(1)} %copy-done.4, bf16[128,1024]{1,0:T(8,128)(2,1)S(1)} %copy-done.6, f32[128,1024]{1,0:T(8,128)S(1)} %get-tuple-element.224.grad_ref, f32[3,1024]{1,0:T(4,128)S(1)} %copy-done.3), custom_call_target="tpu_custom_call" | custom-call | flops 6300000256 | bytes 1048576 | tf_op jit(solution)/shard_map/input_back/pallas_call | solution.py:734
  225.6 1.6 convert_add_fusion
  228.2 2.5 convolution_convert_fusion.2
  234.2 4.3 %all-to-all-start.6 = ((bf16[4,1376,128]{2,1,0:T(8,128)(2,1)}), bf16[4,1376,128]{2,1,0:T(8,128)(2,1)}, u32[]{:S(2)}, u32[]{:S(2)}) async-start(bf16[4,1376,128]{2,1,0:T(8,128)(2,1)} %bitcast.253), calls=%async_computation.6 | async-start | bytes 2818048 | tf_op jit(solution)/shard_map/all_to_all | solution.py:958
  238.5 2.0 collective-permute-start.16
  244.3 7.1 %collective-permute-done.10 = bf16[2,136,1280]{2,1,0:T(8,128)(2,1)} collective-permute-done((bf16[2,136,1280]{2,1,0:T(8,128)(2,1)}, bf16[2,136,1280]{2,1,0:T(8,128)(2,1)}, u32[]{:S(2)}, u32[]{:S(2)}) %collective-permute-start.10) | collective-permute-done | bytes 696352 | tf_op jit(solution)/shard_map/ppermute | solution.py:57
  254.4 3.1 all-to-all-done.6
  257.5 1.7 reduce_sum.215
  259.2 3.8 %collective-permute-done.9 = bf16[2,136,768]{2,1,0:T(8,128)(2,1)} collective-permute-done((bf16[2,136,768]{2,1,0:T(8,128)(2,1)S(1)}, bf16[2,136,768]{2,1,0:T(8,128)(2,1)}, u32[]{:S(2)}, u32[]{:S(2)}) %collective-permute-start.9) | collective-permute-done | bytes 417824 | tf_op jit(solution)/shard_map/ppermute | solution.py:57
  263.0 1.7 collective-permute-start.12
  267.4 1.8 collective-permute-start.14
  273.0 3.6 %collective-permute-done.15 = bf16[1,136,1280]{2,1,0:T(8,128)(2,1)} collective-permute-done((bf16[1,136,1280]{2,1,0:T(8,128)(2,1)}, bf16[1,136,1280]{2,1,0:T(8,128)(2,1)}, u32[]{:S(2)}, u32[]{:S(2)}) %collective-permute-start.15) | collective-permute-done | bytes 348192 | tf_op jit(solution)/shard_map/ppermute | solution.py:57
  277.6 2.9 collective-permute-start.22
  280.5 1.9 collective-permute-start.23
  282.4 2.3 collective-permute-start.24
  287.3 2.5 collective-permute-start.20
  291.6 12.0 %collective-permute-done.23 = bf16[136,1280]{1,0:T(8,128)(2,1)S(1)} collective-permute-done((bf16[136,1280]{1,0:T(8,128)(2,1)S(1)}, bf16[136,1280]{1,0:T(8,128)(2,1)S(1)}, u32[]{:S(2)}, u32[]{:S(2)}) %collective-permute-start.23) | collective-permute-done | bytes 348192 | tf_op jit(solution)/shard_map/ppermute | solution.py:57
  (241 shorter events, 65.5 us)
Async XLA Ops:
  7.2 68.5 %copy-start = (bf16[1024,2]{0,1:T(2,128)(2,1)S(1)}, bf16[1024,2]{0,1:T(2,128)(2,1)}, u32[]{:S(2)}) copy-start(bf16[1024,2]{0,1:T(2,128)(2,1)} %param.32) | copy-start | bytes 12292
  7.2 50.1 %all-gather.3.cloned.1.call-start = ((), (), s32[]{:S(2)}) async-start(), calls=%async_computation.7 | async-start | bytes 2359296 | tf_op jit(solution)/shard_map/all_gather | solution.py:804
  7.9 17.5 %copy-start.32 = (bf16[1024,256]{1,0:T(8,128)(2,1)S(1)}, bf16[1024,256]{1,0:T(8,128)(2,1)}, u32[]{:S(2)}) copy-start(bf16[1024,256]{1,0:T(8,128)(2,1)} %proj_one_ref.1) | copy-start | bytes 1572868
  7.9 18.5 %copy-start.33 = (bf16[64,3328]{1,0:T(8,128)(2,1)S(1)}, bf16[64,3328]{1,0:T(8,128)(2,1)}, u32[]{:S(2)}) copy-start(bf16[64,3328]{1,0:T(8,128)(2,1)} %second_ref.1) | copy-start | bytes 1277956
  25.3 137.6 %all-gather.5.cloned.1.call-start = ((), (), s32[]{:S(2)}) async-start(), calls=%async_computation.8 | async-start | bytes 9175040 | tf_op jit(solution)/shard_map/all_gather | solution.py:824
  28.5 9.5 %copy-start.31 = (bf16[1024,64]{0,1:T(8,128)(2,1)S(1)}, bf16[1024,64]{0,1:T(8,128)(2,1)}, u32[]{:S(2)}) copy-start(bf16[1024,64]{0,1:T(8,128)(2,1)} %param.34) | copy-start | bytes 393220
  44.2 14.0 %copy-start.40 = (s32[1024]{0:T(1024)S(1)}, s32[1024]{0:T(1024)}, u32[]{:S(2)}) copy-start(s32[1024]{0:T(1024)} %param.23) | copy-start | bytes 12292
  44.2 15.2 %copy-start.23 = (bf16[1024,320]{0,1:T(8,128)(2,1)S(1)}, bf16[1024,320]{0,1:T(8,128)(2,1)}, u32[]{:S(2)}) copy-start(bf16[1024,320]{0,1:T(8,128)(2,1)} %param.35) | copy-start | bytes 1966084
  60.6 15.1 %copy-start.24 = (bf16[128,1024]{1,0:T(8,128)(2,1)S(1)}, bf16[128,1024]{1,0:T(8,128)(2,1)}, u32[]{:S(2)}) copy-start(bf16[128,1024]{1,0:T(8,128)(2,1)} %get-tuple-element.93) | copy-start | bytes 786436
  60.6 21.6 %copy-start.39 = (s32[128,128]{1,0:T(8,128)S(1)}, s32[128,128]{1,0:T(8,128)}, u32[]{:S(2)}) copy-start(s32[128,128]{1,0:T(8,128)} %param.41) | copy-start | bytes 196612
  60.6 26.8 %copy-start.14 = (f32[128,1024]{1,0:T(8,128)S(1)}, f32[128,1024]{1,0:T(8,128)}, u32[]{:S(2)}) copy-start(f32[128,1024]{1,0:T(8,128)} %get-tuple-element.102) | copy-start | bytes 1572868
  72.3 9.7 %all-to-all-start = ((f32[8,24,128]{2,1,0:T(8,128)}), f32[8,24,128]{2,1,0:T(8,128)S(1)}, u32[]{:S(2)}, u32[]{:S(2)}) async-start(f32[8,24,128]{2,1,0:T(8,128)} %get-tuple-element.101), calls=%async_computation | async-start | bytes 196608 | tf_op jit(solution)/shard_map/all_to_all | solution.py:841
  83.8 9.6 %all-to-all-start.1 = ((f32[8,24,128]{2,1,0:T(8,128)}), f32[8,24,128]{2,1,0:T(8,128)S(1)}, u32[]{:S(2)}, u32[]{:S(2)}) async-start(f32[8,24,128]{2,1,0:T(8,128)} %pad_maximum_fusion.5), calls=%async_computation.1 | async-start | bytes 196608 | tf_op jit(solution)/shard_map/all_to_all | solution.py:877
  94.1 18.0 %copy-start.13 = (f32[128,1024]{1,0:T(8,128)S(1)}, f32[128,1024]{1,0:T(8,128)}, u32[]{:S(2)}) copy-start(f32[128,1024]{1,0:T(8,128)} %get-tuple-element.110) | copy-start | bytes 1572868
  94.1 18.4 %copy-start.3 = (f32[3,1024]{1,0:T(4,128)S(1)}, f32[3,1024]{1,0:T(4,128)}, u32[]{:S(2)}) copy-start(f32[3,1024]{1,0:T(4,128)} %gains_ref.3) | copy-start | bytes 36868
  112.0 2.9 collective-permute-start
  117.6 31.8 %all-to-all-start.2 = ((bf16[4,128,1024]{2,1,0:T(8,128)(2,1)}), bf16[4,128,1024]{2,1,0:T(8,128)(2,1)S(1)}, u32[]{:S(2)}, u32[]{:S(2)}) async-start(bf16[4,128,1024]{2,1,0:T(8,128)(2,1)} %add_convert_fusion), calls=%async_computation.2 | async-start | bytes 2097152 | tf_op jit(solution)/shard_map/all_to_all | solution.py:894
  131.8 10.5 %collective-permute-start.3 = (bf16[8,32,320]{2,1,0:T(8,128)(2,1)}, bf16[8,32,320]{2,1,0:T(8,128)(2,1)}, u32[]{:S(2)}, u32[]{:S(2)}) collective-permute-start(bf16[8,32,320]{2,1,0:T(8,128)(2,1)} %get-tuple-element.266), channel_id=1, source_target_pairs={{0,8},{8,0},{16,24},{24,16},{1,9},{9,1},{17,25},{25,17},{2,10},{10... | collective-permute-start | bytes 491528 | tf_op jit(solution)/shard_map/ppermute | solution.py:57
  132.9 9.4 %collective-permute-start.4 = (bf16[8,32,320]{2,1,0:T(8,128)(2,1)}, bf16[8,32,320]{2,1,0:T(8,128)(2,1)}, u32[]{:S(2)}, u32[]{:S(2)}) collective-permute-start(bf16[8,32,320]{2,1,0:T(8,128)(2,1)} %get-tuple-element.268), channel_id=1, source_target_pairs={{0,16},{8,24},{16,0},{24,8},{1,17},{9,25},{17,1},{25,9},{2,18},{10... | collective-permute-start | bytes 491528 | tf_op jit(solution)/shard_map/ppermute | solution.py:57
  134.4 12.8 %collective-permute-start.5 = (bf16[8,32,320]{2,1,0:T(8,128)(2,1)}, bf16[8,32,320]{2,1,0:T(8,128)(2,1)}, u32[]{:S(2)}, u32[]{:S(2)}) collective-permute-start(bf16[8,32,320]{2,1,0:T(8,128)(2,1)} %get-tuple-element.267), channel_id=1, source_target_pairs={{0,24},{8,16},{16,8},{24,0},{1,25},{9,17},{17,9},{25,1},{2,26},{10... | collective-permute-start | bytes 491528 | tf_op jit(solution)/shard_map/ppermute | solution.py:57
  152.1 10.9 %all-to-all-start.3 = ((bf16[4,128,256]{2,1,0:T(8,128)(2,1)}), bf16[4,128,256]{2,1,0:T(8,128)(2,1)S(1)}, u32[]{:S(2)}, u32[]{:S(2)}) async-start(bf16[4,128,256]{2,1,0:T(8,128)(2,1)} %bitcast.233), calls=%async_computation.3 | async-start | bytes 524288 | tf_op jit(solution)/shard_map/all_to_all | solution.py:129
  167.8 13.3 %collective-permute-start.1 = (bf16[4,512,256]{2,1,0:T(8,128)(2,1)S(1)}, bf16[4,512,256]{2,1,0:T(8,128)(2,1)}, u32[]{:S(2)}, u32[]{:S(2)}) collective-permute-start(bf16[4,512,256]{2,1,0:T(8,128)(2,1)S(1)} %dynamic-slice_bitcast_fusion.1), channel_id=1, source_target_pairs={{0,1},{1,0},{2,3},{3,2},{4,5},{5,4},{6,7},{7,6},{8,9},{9,8},{10,11... | collective-permute-start | bytes 3145736 | tf_op jit(solution)/shard_map/ppermute | solution.py:57
  167.9 6.5 %copy-start.26 = (f32[128,1024]{1,0:T(8,128)S(1)}, f32[128,1024]{1,0:T(8,128)}, u32[]{:S(2)}) copy-start(f32[128,1024]{1,0:T(8,128)} %get-tuple-element.227) | copy-start | bytes 1572868
  176.8 21.8 %all-to-all-start.4 = ((bf16[4,128,1280]{2,1,0:T(8,128)(2,1)}), bf16[4,128,1280]{2,1,0:T(8,128)(2,1)}, u32[]{:S(2)}, u32[]{:S(2)}) async-start(bf16[4,128,1280]{2,1,0:T(8,128)(2,1)} %pad_maximum_fusion.4), calls=%async_computation.4 | async-start | bytes 2621440 | tf_op jit(solution)/shard_map/all_to_all | solution.py:951
  184.0 19.1 %collective-permute-start.2 = (bf16[2,512,256]{2,1,0:T(8,128)(2,1)}, bf16[2,512,256]{2,1,0:T(8,128)(2,1)}, u32[]{:S(2)}, u32[]{:S(2)}) collective-permute-start(bf16[2,512,256]{2,1,0:T(8,128)(2,1)} %fusion.11), channel_id=1, source_target_pairs={{0,2},{2,0},{4,6},{6,4},{1,3},{3,1},{5,7},{7,5},{8,10},{10,8},{12,... | collective-permute-start | bytes 1572872 | tf_op jit(solution)/shard_map/ppermute | solution.py:57
  198.6 17.8 %all-to-all-start.5 = ((bf16[4,128,768]{2,1,0:T(8,128)(2,1)}), bf16[4,128,768]{2,1,0:T(8,128)(2,1)}, u32[]{:S(2)}, u32[]{:S(2)}) async-start(bf16[4,128,768]{2,1,0:T(8,128)(2,1)} %get-tuple-element.132.parts_ref), calls=%async_computation.5 | async-start | bytes 1572864 | tf_op jit(solution)/shard_map/all_to_all | solution.py:956
  207.6 17.9 %collective-permute-start.7 = (bf16[1,512,256]{2,1,0:T(8,128)(2,1)S(1)}, bf16[1,512,256]{2,1,0:T(8,128)(2,1)S(1)}, u32[]{:S(2)}, u32[]{:S(2)}) collective-permute-start(bf16[1,512,256]{2,1,0:T(8,128)(2,1)S(1)} %dynamic-slice_convert_fusion.3), channel_id=1, source_target_pairs={{0,4},{2,6},{4,0},{6,2},{1,5},{3,7},{5,1},{7,3},{8,12},{10,14},{12... | collective-permute-start | bytes 786440 | tf_op jit(solution)/shard_map/ppermute | solution.py:57
  216.3 9.3 %collective-permute-start.6 = (bf16[4,136,1280]{2,1,0:T(8,128)(2,1)S(1)}, bf16[4,136,1280]{2,1,0:T(8,128)(2,1)}, u32[]{:S(2)}, u32[]{:S(2)}) collective-permute-start(bf16[4,136,1280]{2,1,0:T(8,128)(2,1)S(1)} %dynamic-slice_bitcast_fusion), channel_id=1, source_target_pairs={{0,1},{1,0},{2,3},{3,2},{4,5},{5,4},{6,7},{7,6},{8,9},{9,8},{10,11... | collective-permute-start | bytes 4177928 | tf_op jit(solution)/shard_map/ppermute | solution.py:57
  232.7 9.4 %collective-permute-start.8 = (bf16[4,136,768]{2,1,0:T(8,128)(2,1)}, bf16[4,136,768]{2,1,0:T(8,128)(2,1)}, u32[]{:S(2)}, u32[]{:S(2)}) collective-permute-start(bf16[4,136,768]{2,1,0:T(8,128)(2,1)} %fusion.7), channel_id=1, source_target_pairs={{0,1},{1,0},{2,3},{3,2},{4,5},{5,4},{6,7},{7,6},{8,9},{9,8},{10,11... | collective-permute-start | bytes 2506760 | tf_op jit(solution)/shard_map/ppermute | solution.py:57
  232.7 18.7 %collective-permute-start.10 = (bf16[2,136,1280]{2,1,0:T(8,128)(2,1)}, bf16[2,136,1280]{2,1,0:T(8,128)(2,1)}, u32[]{:S(2)}, u32[]{:S(2)}) collective-permute-start(bf16[2,136,1280]{2,1,0:T(8,128)(2,1)} %fusion.10), channel_id=1, source_target_pairs={{0,2},{2,0},{4,6},{6,4},{1,3},{3,1},{5,7},{7,5},{8,10},{10,8},{12,... | collective-permute-start | bytes 2088968 | tf_op jit(solution)/shard_map/ppermute | solution.py:57
  234.2 23.3 %all-to-all-start.6 = ((bf16[4,1376,128]{2,1,0:T(8,128)(2,1)}), bf16[4,1376,128]{2,1,0:T(8,128)(2,1)}, u32[]{:S(2)}, u32[]{:S(2)}) async-start(bf16[4,1376,128]{2,1,0:T(8,128)(2,1)} %bitcast.253), calls=%async_computation.6 | async-start | bytes 2818048 | tf_op jit(solution)/shard_map/all_to_all | solution.py:958
  238.5 27.3 %collective-permute-start.16 = (bf16[512,256]{1,0:T(8,128)(2,1)S(1)}, bf16[512,256]{1,0:T(8,128)(2,1)}, u32[]{:S(2)}, u32[]{:S(2)}) collective-permute-start(bf16[512,256]{1,0:T(8,128)(2,1)S(1)} %fusion.17), channel_id=1, source_target_pairs={{0,8},{8,0},{16,24},{24,16},{1,9},{9,1},{17,25},{25,17},{2,10},{10... | collective-permute-start | bytes 786440 | tf_op jit(solution)/shard_map/ppermute | solution.py:57
  240.5 26.9 %collective-permute-start.17 = (bf16[512,256]{1,0:T(8,128)(2,1)S(1)}, bf16[512,256]{1,0:T(8,128)(2,1)}, u32[]{:S(2)}, u32[]{:S(2)}) collective-permute-start(bf16[512,256]{1,0:T(8,128)(2,1)S(1)} %fusion.17), channel_id=1, source_target_pairs={{0,16},{8,24},{16,0},{24,8},{1,17},{9,25},{17,1},{25,9},{2,18},{10... | collective-permute-start | bytes 786440 | tf_op jit(solution)/shard_map/ppermute | solution.py:57
  242.0 27.6 %collective-permute-start.18 = (bf16[512,256]{1,0:T(8,128)(2,1)S(1)}, bf16[512,256]{1,0:T(8,128)(2,1)}, u32[]{:S(2)}, u32[]{:S(2)}) collective-permute-start(bf16[512,256]{1,0:T(8,128)(2,1)S(1)} %fusion.17), channel_id=1, source_target_pairs={{0,24},{8,16},{16,8},{24,0},{1,25},{9,17},{17,9},{25,1},{2,26},{10... | collective-permute-start | bytes 786440 | tf_op jit(solution)/shard_map/ppermute | solution.py:57
  243.7 9.0 %copy-start.16 = (f32[4,136,768]{2,1,0:T(8,128)}, f32[4,136,768]{2,1,0:T(8,128)S(1)}, u32[]{:S(2)}) copy-start(f32[4,136,768]{2,1,0:T(8,128)S(1)} %convert_add_fusion.2) | copy-start | bytes 5013508
  243.7 19.3 %collective-permute-start.9 = (bf16[2,136,768]{2,1,0:T(8,128)(2,1)S(1)}, bf16[2,136,768]{2,1,0:T(8,128)(2,1)}, u32[]{:S(2)}, u32[]{:S(2)}) collective-permute-start(bf16[2,136,768]{2,1,0:T(8,128)(2,1)S(1)} %fusion.12), channel_id=1, source_target_pairs={{0,2},{2,0},{4,6},{6,4},{1,3},{3,1},{5,7},{7,5},{8,10},{10,8},{12,... | collective-permute-start | bytes 1253384 | tf_op jit(solution)/shard_map/ppermute | solution.py:57
  253.9 10.8 %copy-start.17 = (f32[4,136,768]{2,1,0:T(8,128)S(1)}, f32[4,136,768]{2,1,0:T(8,128)}, u32[]{:S(2)}) copy-start(f32[4,136,768]{2,1,0:T(8,128)} %copy-done.16) | copy-start | bytes 5013508
  253.9 22.6 %collective-permute-start.15 = (bf16[1,136,1280]{2,1,0:T(8,128)(2,1)}, bf16[1,136,1280]{2,1,0:T(8,128)(2,1)}, u32[]{:S(2)}, u32[]{:S(2)}) collective-permute-start(bf16[1,136,1280]{2,1,0:T(8,128)(2,1)} %dynamic-slice_convert_fusion.2), channel_id=1, source_target_pairs={{0,4},{2,6},{4,0},{6,2},{1,5},{3,7},{5,1},{7,3},{8,12},{10,14},{12... | collective-permute-start | bytes 1044488 | tf_op jit(solution)/shard_map/ppermute | solution.py:57
  263.0 17.5 %collective-permute-start.12 = (bf16[1376,128]{1,0:T(8,128)(2,1)S(1)}, bf16[1376,128]{1,0:T(8,128)(2,1)S(1)}, u32[]{:S(2)}, u32[]{:S(2)}) collective-permute-start(bf16[1376,128]{1,0:T(8,128)(2,1)S(1)} %reduce_sum.215), channel_id=1, source_target_pairs={{0,8},{8,0},{16,24},{24,16},{1,9},{9,1},{17,25},{25,17},{2,10},{10... | collective-permute-start | bytes 1056776 | tf_op jit(solution)/shard_map/ppermute | solution.py:57
  265.9 16.6 %collective-permute-start.13 = (bf16[1376,128]{1,0:T(8,128)(2,1)S(1)}, bf16[1376,128]{1,0:T(8,128)(2,1)S(1)}, u32[]{:S(2)}, u32[]{:S(2)}) collective-permute-start(bf16[1376,128]{1,0:T(8,128)(2,1)S(1)} %reduce_sum.215), channel_id=1, source_target_pairs={{0,16},{8,24},{16,0},{24,8},{1,17},{9,25},{17,1},{25,9},{2,18},{10... | collective-permute-start | bytes 1056776 | tf_op jit(solution)/shard_map/ppermute | solution.py:57
  267.4 17.3 %collective-permute-start.14 = (bf16[1376,128]{1,0:T(8,128)(2,1)S(1)}, bf16[1376,128]{1,0:T(8,128)(2,1)S(1)}, u32[]{:S(2)}, u32[]{:S(2)}) collective-permute-start(bf16[1376,128]{1,0:T(8,128)(2,1)S(1)} %reduce_sum.215), channel_id=1, source_target_pairs={{0,24},{8,16},{16,8},{24,0},{1,25},{9,17},{17,9},{25,1},{2,26},{10... | collective-permute-start | bytes 1056776 | tf_op jit(solution)/shard_map/ppermute | solution.py:57
  269.6 16.9 %collective-permute-start.11 = (bf16[1,136,768]{2,1,0:T(8,128)(2,1)S(1)}, bf16[1,136,768]{2,1,0:T(8,128)(2,1)S(1)}, u32[]{:S(2)}, u32[]{:S(2)}) collective-permute-start(bf16[1,136,768]{2,1,0:T(8,128)(2,1)S(1)} %dynamic-slice_convert_fusion.4), channel_id=1, source_target_pairs={{0,4},{2,6},{4,0},{6,2},{1,5},{3,7},{5,1},{7,3},{8,12},{10,14},{12... | collective-permute-start | bytes 626696 | tf_op jit(solution)/shard_map/ppermute | solution.py:57
  277.6 13.6 %collective-permute-start.22 = (bf16[136,1280]{1,0:T(8,128)(2,1)S(1)}, bf16[136,1280]{1,0:T(8,128)(2,1)S(1)}, u32[]{:S(2)}, u32[]{:S(2)}) collective-permute-start(bf16[136,1280]{1,0:T(8,128)(2,1)S(1)} %fusion.16), channel_id=1, source_target_pairs={{0,8},{8,0},{16,24},{24,16},{1,9},{9,1},{17,25},{25,17},{2,10},{10... | collective-permute-start | bytes 1044488 | tf_op jit(solution)/shard_map/ppermute | solution.py:57
  280.5 23.0 %collective-permute-start.23 = (bf16[136,1280]{1,0:T(8,128)(2,1)S(1)}, bf16[136,1280]{1,0:T(8,128)(2,1)S(1)}, u32[]{:S(2)}, u32[]{:S(2)}) collective-permute-start(bf16[136,1280]{1,0:T(8,128)(2,1)S(1)} %fusion.16), channel_id=1, source_target_pairs={{0,16},{8,24},{16,0},{24,8},{1,17},{9,25},{17,1},{25,9},{2,18},{10... | collective-permute-start | bytes 1044488 | tf_op jit(solution)/shard_map/ppermute | solution.py:57
  282.4 21.1 %collective-permute-start.24 = (bf16[136,1280]{1,0:T(8,128)(2,1)S(1)}, bf16[136,1280]{1,0:T(8,128)(2,1)S(1)}, u32[]{:S(2)}, u32[]{:S(2)}) collective-permute-start(bf16[136,1280]{1,0:T(8,128)(2,1)S(1)} %fusion.16), channel_id=1, source_target_pairs={{0,24},{8,16},{16,8},{24,0},{1,25},{9,17},{17,9},{25,1},{2,26},{10... | collective-permute-start | bytes 1044488 | tf_op jit(solution)/shard_map/ppermute | solution.py:57
  286.6 21.3 %collective-permute-start.19 = (bf16[136,768]{1,0:T(8,128)(2,1)S(1)}, bf16[136,768]{1,0:T(8,128)(2,1)S(1)}, u32[]{:S(2)}, u32[]{:S(2)}) collective-permute-start(bf16[136,768]{1,0:T(8,128)(2,1)S(1)} %bitcast.259), channel_id=1, source_target_pairs={{0,24},{8,16},{16,8},{24,0},{1,25},{9,17},{17,9},{25,1},{2,26},{10... | collective-permute-start | bytes 626696 | tf_op jit(solution)/shard_map/ppermute | solution.py:57
  287.3 20.6 %collective-permute-start.20 = (bf16[136,768]{1,0:T(8,128)(2,1)S(1)}, bf16[136,768]{1,0:T(8,128)(2,1)S(1)}, u32[]{:S(2)}, u32[]{:S(2)}) collective-permute-start(bf16[136,768]{1,0:T(8,128)(2,1)S(1)} %bitcast.260), channel_id=1, source_target_pairs={{0,16},{8,24},{16,0},{24,8},{1,17},{9,25},{17,1},{25,9},{2,18},{10... | collective-permute-start | bytes 626696 | tf_op jit(solution)/shard_map/ppermute | solution.py:57
  291.2 16.7 %collective-permute-start.21 = (bf16[136,768]{1,0:T(8,128)(2,1)S(1)}, bf16[136,768]{1,0:T(8,128)(2,1)S(1)}, u32[]{:S(2)}, u32[]{:S(2)}) collective-permute-start(bf16[136,768]{1,0:T(8,128)(2,1)S(1)} %bitcast.261), channel_id=1, source_target_pairs={{0,8},{8,0},{16,24},{24,16},{1,9},{9,1},{17,25},{25,17},{2,10},{10... | collective-permute-start | bytes 626696 | tf_op jit(solution)/shard_map/ppermute | solution.py:57
  (28 other events, 74.5 us)
Sparse Core Ops, SparseCore 0:
  25.4 31.7 all-gather.2
  59.7 81.3 all-gather.4
